TPU v7x, 32 devices: a whole 2x2x4 slice. The times are simulated.
32 devices in a mesh: gx: 8 (over z, x), gy: 4 (over y, core).
Axes of the slice: x: 2, y: 2, z: 4, core: 2. Of those that a mesh axis runs over, the one named last changes fastest.
Arguments:
- tangent: float32 [128, 64, 512], P('gx', 'gy'), may hold values from -6 to 6
- hessian: bfloat16 [5, 5, 128, 64, 512], P(None, None, 'gx', 'gy'), may hold values from -1.5 to 8, as said below
- kernel_rows: float32 [5, 17], replicated, may hold values from -1 to 1
- kernel_cols: float32 [5, 17], replicated, may hold values from -1 to 1
- kernel_depth: bfloat16 [5, 17], replicated, may hold values from -1 to 1
Outputs:
- hessian_product: float32 [128, 64, 512], P('gx', 'gy')
Inputs may be any that keep to these rules, and one draw needn't show every extreme that they name: `hessian`: Off-diagonal entries lie within -1.5 to 1.5; diagonal entries are positive, between 0.3 and 8.
All inputs are finite; a program needn't handle non-finite values.
Results may differ from a plain program's by a relative error of at most 0.0022.
Values sent between devices are 32-bit elements; how exact they have to be, the bound alone decides.
A program may use at most 128 MiB of HBM per device.

v0:
```python
import jax
import jax.numpy as jnp
from jax import lax
from jax.sharding import PartitionSpec as P

RADIUS = 8
DENSITIES = 5


def padded(cells, sides, width):
    for axis, dim in sides:
        count = lax.axis_size(axis)
        head = lax.slice_in_dim(cells, 0, width, axis=dim)
        tail = lax.slice_in_dim(cells, cells.shape[dim] - width, cells.shape[dim], axis=dim)
        cells = jnp.concatenate(
            [
                lax.ppermute(tail, axis, [(i, (i + 1) % count) for i in range(count)]),
                cells,
                lax.ppermute(head, axis, [((i + 1) % count, i) for i in range(count)]),
            ],
            axis=dim,
        )
    return cells


def from_behind(block, axis, distance):
    devices = range(lax.axis_size(axis))
    route = [((i - distance) % len(devices), i) for i in devices]
    return lax.ppermute(block, axis, route)


def depth_bands(kernel_depth, depth):
    rows_index = lax.broadcasted_iota(jnp.int32, (depth, depth), 0)
    cols_index = lax.broadcasted_iota(jnp.int32, (depth, depth), 1)
    offsets = cols_index - rows_index
    weights = kernel_depth.astype(jnp.float32)
    bands = []
    for density in range(DENSITIES):
        matrix = jnp.zeros((depth, depth), jnp.float32)
        for shift_tap in range(2 * RADIUS + 1):
            matrix = matrix + jnp.where(
                offsets == shift_tap - RADIUS, weights[density, shift_tap], 0.0
            )
        bands.append(matrix.astype(jnp.bfloat16))
    return bands


def per_device(tangent, hessian, kernel_rows, kernel_cols, kernel_depth):
    span_rows, span_cols, depth = tangent.shape
    reach = RADIUS
    extended = padded(tangent, (("gx", 0), ("gy", 1)), RADIUS)
    bands = depth_bands(kernel_depth, depth)
    densities = []
    for density in range(DENSITIES):
        along_rows = jnp.zeros((span_rows, span_cols + 2 * reach, depth), jnp.float32)
        for shift_tap in range(2 * reach + 1):
            along_rows = (
                along_rows
                + kernel_rows[density, shift_tap] * extended[shift_tap : shift_tap + span_rows]
            )
        along_cols = jnp.zeros((span_rows, span_cols, depth), jnp.float32)
        for shift_tap in range(2 * reach + 1):
            along_cols = (
                along_cols
                + kernel_cols[density, shift_tap] * along_rows[:, shift_tap : shift_tap + span_cols]
            )
        lowered = along_cols.astype(jnp.bfloat16).reshape(-1, depth)
        flat = jnp.dot(lowered, bands[density].T, preferred_element_type=jnp.float32)
        densities.append(flat.reshape(span_rows, span_cols, depth))
    transformed = []
    for density in range(DENSITIES):
        gradient = jnp.zeros((span_rows, span_cols, depth), jnp.float32)
        for other in range(DENSITIES):
            gradient = gradient + hessian[density, other].astype(jnp.float32) * densities[other]
        lowered = gradient.astype(jnp.bfloat16).reshape(-1, depth)
        flat = jnp.dot(lowered, bands[density], preferred_element_type=jnp.float32)
        transformed.append(flat.reshape(span_rows, span_cols, depth))
    stacked = jnp.stack(transformed, 0)
    row_weights = kernel_rows[:, :, None, None, None]
    col_weights = kernel_cols[:, :, None, None, None]
    spread_rows = jnp.zeros((DENSITIES, span_rows + 2 * reach, span_cols, depth), jnp.float32)
    for shift_tap in range(2 * reach + 1):
        spread_rows = spread_rows + jnp.pad(
            row_weights[:, shift_tap] * stacked,
            ((0, 0), (shift_tap, 2 * reach - shift_tap), (0, 0), (0, 0)),
        )
    spread_both = jnp.zeros(
        (DENSITIES, span_rows + 2 * reach, span_cols + 2 * reach, depth), jnp.float32
    )
    for shift_tap in range(2 * reach + 1):
        spread_both = spread_both + jnp.pad(
            col_weights[:, shift_tap] * spread_rows,
            ((0, 0), (0, 0), (shift_tap, 2 * reach - shift_tap), (0, 0)),
        )
    spread = jnp.sum(spread_both, 0)
    middle = spread[reach : reach + span_rows]
    from_next = from_behind(spread[:reach], "gx", -1)
    from_prev = from_behind(spread[span_rows + reach :], "gx", 1)
    middle = middle.at[span_rows - reach :].add(from_next)
    middle = middle.at[:reach].add(from_prev)
    center = middle[:, reach : reach + span_cols]
    from_right = from_behind(middle[:, :reach], "gy", -1)
    from_left = from_behind(middle[:, span_cols + reach :], "gy", 1)
    center = center.at[:, span_cols - reach :].add(from_right)
    center = center.at[:, :reach].add(from_left)
    return center


def solution(mesh):
    return jax.shard_map(
        per_device,
        mesh=mesh,
        in_specs=(P("gx", "gy", None), P(None, None, "gx", "gy", None), P(), P(), P()),
        out_specs=P("gx", "gy", None),
        check_vma=False,
    )
```

profile of v0, /device:TPU:0, one launch (start us, length us, event | category | flops | bytes accessed | tf_op | source)
XLA Modules:
  0.0 415.3 jit_solution(11542406116270865392)
XLA Ops:
  0.0 1.1 fusion.429
  1.1 6.1 %collective-permute-start.1 = (f32[8,16,512]{2,1,0:T(8,128)S(1)}, f32[8,16,512]{2,1,0:T(8,128)S(1)}, u32[]{:S(2)}, u32[]{:S(2)}) collective-permute-start(f32[8,16,512]{2,1,0:T(8,128)S(1)} %get-tuple-element.128), channel_id=1, source_target_pairs={{4,0},{8,4},{12,8},{16,12},{20,16},{24,20},{28,24},{0,28},{5,1},{9... | collective-permute-start | bytes 786440 | tf_op jit(solution)/shard_map/ppermute | solution.py:19
  7.2 2.1 fusion.443
  9.3 2.1 fusion.441
  11.4 2.1 fusion.440
  13.5 2.1 fusion.437
  15.6 2.1 fusion.438
  17.7 2.1 fusion.432
  19.8 2.1 fusion.433
  21.9 1.8 slice_reduce_fusion.33
  23.7 1.8 slice_reduce_fusion.32
  25.5 1.7 fusion.439
  27.2 2.1 fusion.436
  29.3 1.7 fusion.434
  31.0 1.1 constant_dynamic-update-slice_fusion.1
  32.3 1.7 collective-permute-start.3
  34.7 0.7 fusion.431
  35.5 0.7 fusion.442
  36.2 0.7 fusion.435
  36.9 0.7 fusion.430
  37.6 7.1 %collective-permute-done.2 = f32[32,8,512]{2,1,0:T(8,128)S(1)} collective-permute-done((f32[32,8,512]{2,1,0:T(8,128)S(1)}, f32[32,8,512]{2,1,0:T(8,128)S(1)}, u32[]{:S(2)}, u32[]{:S(2)}) %collective-permute-start.2) | collective-permute-done | bytes 524320 | tf_op jit(solution)/shard_map/ppermute | solution.py:17
  44.7 0.9 collective-permute-done.3
  45.8 13.0 %multiply_add_fusion.2 = f32[16,32,512]{2,1,0:T(8,128)S(1)} fusion(f32[32,32,512]{2,1,0:T(8,128)S(1)} %pad_maximum_fusion, f32[]{:T(128)} %bitcast.126, f32[]{:T(128)} %bitcast.125, f32[]{:T(128)} %bitcast.124, f32[]{:T(128)} %bitcast.123, f32[]{:T(128)} %bitcast.122, f32[]{:T(128)} %bitcast.121, f32[]{:T(128)} %bitcast.120, f32[]{:T(128)} %bitcast.119, ...), kind=kLoop, calls=%fused_computation.52 | loop fusion | flops 8650752 | bytes 18874436 | tf_op jit(solution)/shard_map/add | solution.py:58
  58.9 12.8 %multiply_add_fusion.1 = f32[16,32,512]{2,1,0:T(8,128)S(1)} fusion(f32[32,32,512]{2,1,0:T(8,128)S(1)} %pad_maximum_fusion, f32[]{:T(128)} %bitcast.179, f32[]{:T(128)} %bitcast.178, f32[]{:T(128)} %bitcast.177, f32[]{:T(128)} %bitcast.176, f32[]{:T(128)} %bitcast.175, f32[]{:T(128)} %bitcast.174, f32[]{:T(128)} %bitcast.173, f32[]{:T(128)} %bitcast.172, ...), kind=kLoop, calls=%fused_computation.50 | loop fusion | flops 8650752 | bytes 18874436 | tf_op jit(solution)/shard_map/add | solution.py:58
  71.7 12.8 %multiply_add_fusion = f32[16,32,512]{2,1,0:T(8,128)S(1)} fusion(f32[32,32,512]{2,1,0:T(8,128)S(1)} %pad_maximum_fusion, f32[]{:T(128)} %bitcast.232, f32[]{:T(128)} %bitcast.231, f32[]{:T(128)} %bitcast.230, f32[]{:T(128)} %bitcast.229, f32[]{:T(128)} %bitcast.228, f32[]{:T(128)} %bitcast.227, f32[]{:T(128)} %bitcast.226, f32[]{:T(128)} %bitcast.225, ...), kind=kLoop, calls=%fused_computation.48 | loop fusion | flops 8650752 | bytes 18874436 | tf_op jit(solution)/shard_map/add | solution.py:58
  84.6 12.7 %multiply_add_fusion.4 = f32[16,32,512]{2,1,0:T(8,128)S(1)} fusion(f32[32,32,512]{2,1,0:T(8,128)S(1)} %pad_maximum_fusion, f32[]{:T(128)} %bitcast.20, f32[]{:T(128)} %bitcast.19, f32[]{:T(128)} %bitcast.18, f32[]{:T(128)} %bitcast.17, f32[]{:T(128)} %bitcast.16, f32[]{:T(128)} %bitcast.15, f32[]{:T(128)} %bitcast.14, f32[]{:T(128)} %bitcast.13, ...), kind=kLoop, calls=%fused_computation.74 | loop fusion | flops 8650752 | bytes 18874436 | tf_op jit(solution)/shard_map/add | solution.py:58
  97.3 13.0 %multiply_add_fusion.3 = f32[16,32,512]{2,1,0:T(8,128)S(1)} fusion(f32[32,32,512]{2,1,0:T(8,128)S(1)} %pad_maximum_fusion, f32[]{:T(128)} %bitcast.73, f32[]{:T(128)} %bitcast.72, f32[]{:T(128)} %bitcast.71, f32[]{:T(128)} %bitcast.70, f32[]{:T(128)} %bitcast.69, f32[]{:T(128)} %bitcast.68, f32[]{:T(128)} %bitcast.67, f32[]{:T(128)} %bitcast.66, ...), kind=kLoop, calls=%fused_computation.54 | loop fusion | flops 8650752 | bytes 18874436 | tf_op jit(solution)/shard_map/add | solution.py:58
  110.3 22.8 %fusion.146 = f32[16,16,512]{2,1,0:T(8,128)S(1)} fusion(f32[]{:T(128)} %bitcast.159, f32[]{:T(128)} %bitcast.158, f32[]{:T(128)} %bitcast.157, f32[]{:T(128)} %bitcast.156, f32[]{:T(128)} %bitcast.155, f32[]{:T(128)} %bitcast.154, f32[]{:T(128)} %bitcast.153, f32[]{:T(128)} %bitcast.152, f32[]{:T(128)} %bitcast.151, f32[]{:T(128)} %bitcast.150, ...), kind=kOutput, calls=%fused_computation.306 | convolution fusion | flops 152305664 | bytes 9437320 | tf_op jit(solution)/shard_map/dot_general | solution.py:68
  133.1 22.5 %fusion.143 = f32[16,16,512]{2,1,0:T(8,128)S(1)} fusion(f32[]{:T(128)} %bitcast.212, f32[]{:T(128)} %bitcast.211, f32[]{:T(128)} %bitcast.210, f32[]{:T(128)} %bitcast.209, f32[]{:T(128)} %bitcast.208, f32[]{:T(128)} %bitcast.207, f32[]{:T(128)} %bitcast.206, f32[]{:T(128)} %bitcast.205, f32[]{:T(128)} %bitcast.204, f32[]{:T(128)} %bitcast.203, ...), kind=kOutput, calls=%fused_computation.305 | convolution fusion | flops 152305664 | bytes 9437320 | tf_op jit(solution)/shard_map/dot_general | solution.py:68
  155.6 22.6 %fusion.140 = f32[16,16,512]{2,1,0:T(8,128)S(1)} fusion(f32[]{:T(128)} %bitcast.265, f32[]{:T(128)} %bitcast.264, f32[]{:T(128)} %bitcast.263, f32[]{:T(128)} %bitcast.262, f32[]{:T(128)} %bitcast.261, f32[]{:T(128)} %bitcast.260, f32[]{:T(128)} %bitcast.259, f32[]{:T(128)} %bitcast.258, f32[]{:T(128)} %bitcast.257, f32[]{:T(128)} %bitcast.256, ...), kind=kOutput, calls=%fused_computation.304 | convolution fusion | flops 152305664 | bytes 9437320 | tf_op jit(solution)/shard_map/dot_general | solution.py:68
  178.2 22.4 %fusion.149 = f32[16,16,512]{2,1,0:T(8,128)S(1)} fusion(f32[]{:T(128)} %bitcast.106, f32[]{:T(128)} %bitcast.105, f32[]{:T(128)} %bitcast.104, f32[]{:T(128)} %bitcast.103, f32[]{:T(128)} %bitcast.102, f32[]{:T(128)} %bitcast.101, f32[]{:T(128)} %bitcast.100, f32[]{:T(128)} %bitcast.99, f32[]{:T(128)} %bitcast.98, f32[]{:T(128)} %bitcast.97, f32[]{:T(128)} %bitcast.96, ...), kind=kOutput, calls=%fused_computation.307 | convolution fusion | flops 152305664 | bytes 9437320 | tf_op jit(solution)/shard_map/dot_general | solution.py:68
  200.6 23.0 %fusion.160 = f32[16,16,512]{2,1,0:T(8,128)S(1)} fusion(f32[]{:T(128)} %bitcast.53, f32[]{:T(128)} %bitcast.52, f32[]{:T(128)} %bitcast.51, f32[]{:T(128)} %bitcast.50, f32[]{:T(128)} %bitcast.49, f32[]{:T(128)} %bitcast.48, f32[]{:T(128)} %bitcast.47, f32[]{:T(128)} %bitcast.46, f32[]{:T(128)} %bitcast.45, f32[]{:T(128)} %bitcast.44, f32[]{:T(128)} %bitcast.43, ...), kind=kOutput, calls=%fused_computation.316 | convolution fusion | flops 152305664 | bytes 9437320 | tf_op jit(solution)/shard_map/dot_general | solution.py:68
  223.6 12.9 %fusion.4 = f32[5,16,16,512]{3,2,1,0:T(8,128)S(1)} fusion(f32[]{:T(128)} %bitcast.53, f32[]{:T(128)} %bitcast.52, f32[]{:T(128)} %bitcast.51, f32[]{:T(128)} %bitcast.50, f32[]{:T(128)} %bitcast.49, f32[]{:T(128)} %bitcast.48, f32[]{:T(128)} %bitcast.47, f32[]{:T(128)} %bitcast.46, f32[]{:T(128)} %bitcast.45, f32[]{:T(128)} %bitcast.44, f32[]{:T(128)} %bitcast.43, ...), kind=kOutput, calls=%fused_computation.46 | convolution fusion | flops 149815296 | bytes 4465152 | tf_op jit(solution)/shard_map/dot_general | solution.py:76
  236.4 12.6 %fusion.3 = f32[5,16,16,512]{3,2,1,0:T(8,128)S(1)} fusion(f32[5,16,16,512]{3,2,1,0:T(8,128)S(1)} %fusion.4, f32[]{:T(128)} %bitcast.106, f32[]{:T(128)} %bitcast.105, f32[]{:T(128)} %bitcast.104, f32[]{:T(128)} %bitcast.103, f32[]{:T(128)} %bitcast.102, f32[]{:T(128)} %bitcast.101, f32[]{:T(128)} %bitcast.100, f32[]{:T(128)} %bitcast.99, f32[]{:T(128)} %bitcast.98, ...), kind=kOutput, calls=%fused_computation.44 | convolution fusion | flops 149815296 | bytes 4465152 | tf_op jit(solution)/shard_map/dot_general | solution.py:76
  249.0 12.9 %fusion.2 = f32[5,16,16,512]{3,2,1,0:T(8,128)S(1)} fusion(f32[5,16,16,512]{3,2,1,0:T(8,128)S(1)} %fusion.3, f32[]{:T(128)} %bitcast.159, f32[]{:T(128)} %bitcast.158, f32[]{:T(128)} %bitcast.157, f32[]{:T(128)} %bitcast.156, f32[]{:T(128)} %bitcast.155, f32[]{:T(128)} %bitcast.154, f32[]{:T(128)} %bitcast.153, f32[]{:T(128)} %bitcast.152, f32[]{:T(128)} %bitcast.151, ...), kind=kOutput, calls=%fused_computation.42 | convolution fusion | flops 149815296 | bytes 4465152 | tf_op jit(solution)/shard_map/dot_general | solution.py:76
  261.9 12.9 %fusion.1 = f32[5,16,16,512]{3,2,1,0:T(8,128)S(1)} fusion(f32[5,16,16,512]{3,2,1,0:T(8,128)S(1)} %fusion.2, f32[]{:T(128)} %bitcast.212, f32[]{:T(128)} %bitcast.211, f32[]{:T(128)} %bitcast.210, f32[]{:T(128)} %bitcast.209, f32[]{:T(128)} %bitcast.208, f32[]{:T(128)} %bitcast.207, f32[]{:T(128)} %bitcast.206, f32[]{:T(128)} %bitcast.205, f32[]{:T(128)} %bitcast.204, ...), kind=kOutput, calls=%fused_computation.40 | convolution fusion | flops 149815296 | bytes 4465152 | tf_op jit(solution)/shard_map/dot_general | solution.py:76
  274.8 12.7 %fusion = f32[5,16,16,512]{3,2,1,0:T(8,128)S(1)} fusion(f32[5,16,16,512]{3,2,1,0:T(8,128)S(1)} %fusion.1, f32[]{:T(128)} %bitcast.265, f32[]{:T(128)} %bitcast.264, f32[]{:T(128)} %bitcast.263, f32[]{:T(128)} %bitcast.262, f32[]{:T(128)} %bitcast.261, f32[]{:T(128)} %bitcast.260, f32[]{:T(128)} %bitcast.259, f32[]{:T(128)} %bitcast.258, f32[]{:T(128)} %bitcast.257, ...), kind=kOutput, calls=%fused_computation.38 | convolution fusion | flops 149815296 | bytes 4465152 | tf_op jit(solution)/shard_map/dot_general | solution.py:76
  287.5 1.5 copy-done.2
  289.0 15.8 %broadcast_multiply_fusion.33 = (f32[5,16,16,512]{3,2,1,0:T(8,128)S(1)}, f32[5,16,16,512]{3,2,1,0:T(8,128)S(1)}, f32[5,16,16,512]{3,2,1,0:T(8,128)S(1)}, f32[5,1...) fusion(f32[5,16,16,512]{3,2,1,0:T(8,128)} %copy-done.2, ...), kind=kLoop, calls=%fused_computation.36 | loop fusion | flops 11141120 | bytes 47186260 | tf_op jit(solution)/shard_map/mul | solution.py:84
  304.8 17.3 %broadcast_multiply_fusion.16 = (f32[5,32,16,512]{3,2,1,0:T(8,128)}, f32[5,32,16,512]{3,2,1,0:T(8,128)}) fusion(f32[5]{0:T(128)S(1)} %get-tuple-element.53, f32[5,16,16,512]{3,2,1,0:T(8,128)S(1)} %get-tuple-element.106, f32[5,16,16,512]{3,2,1,0:T(8,128)S(1)} %get-tuple-element.107, f32[5,16,16,512]{3,2,1,0:T(8,128)} %get-tuple-element.108, ...), kind=kLoop, calls=%fused_computation.18 | loop fusion | flops 22282240 | bytes 55050260 | tf_op jit(solution)/shard_map/mul | solution.py:92
  322.1 27.3 %broadcast_multiply_fusion.15 = (f32[5,32,16,512]{3,2,1,0:T(8,128)S(1)}, f32[5,32,16,512]{3,2,1,0:T(8,128)S(1)}, f32[5,32,16,512]{3,2,1,0:T(8,128)}, f32[5,32,16...) fusion(f32[5,32,16,512]{3,2,1,0:T(8,128)} %get-tuple-element.88, ...), kind=kLoop, calls=%fused_computation.17 | loop fusion | flops 20971520 | bytes 89129280 | tf_op jit(solution)/shard_map/mul | solution.py:92
  349.4 29.1 %add_reduce_fusion = f32[32,32,512]{2,1,0:T(8,128)S(1)} fusion(f32[5,32,16,512]{3,2,1,0:T(8,128)} %get-tuple-element.104, f32[5,32,16,512]{3,2,1,0:T(8,128)S(1)} %get-tuple-element.90, f32[5,32,16,512]{3,2,1,0:T(8,128)} %get-tuple-element.91, f32[5,32,16,512]{3,2,1,0:T(8,128)} %get-tuple-element.92, f32[5,32,16,512]{3,2,1,0:T(8,128)} %get-tuple-element.93, ...), kind=kLoop, calls=%fused_computation | loop fusion | flops 44040192 | bytes 91226112 | tf_op jit(solution)/shard_map/reduce_sum | solution.py:95
  378.6 4.8 %collective-permute-start.4 = (f32[8,32,512]{2,1,0:T(8,128)S(1)}, f32[8,32,512]{2,1,0:T(8,128)S(1)}, u32[]{:S(2)}, u32[]{:S(2)}) collective-permute-start(f32[8,32,512]{2,1,0:T(8,128)S(1)} %get-tuple-element.123), channel_id=1, source_target_pairs={{4,0},{8,4},{12,8},{16,12},{20,16},{24,20},{28,24},{0,28},{5,1},{9... | collective-permute-start | bytes 1572872 | tf_op jit(solution)/shard_map/ppermute | solution.py:29
  383.5 21.0 %collective-permute-done.4 = f32[8,32,512]{2,1,0:T(8,128)S(1)} collective-permute-done((f32[8,32,512]{2,1,0:T(8,128)S(1)}, f32[8,32,512]{2,1,0:T(8,128)S(1)}, u32[]{:S(2)}, u32[]{:S(2)}) %collective-permute-start.4) | collective-permute-done | bytes 524320 | tf_op jit(solution)/shard_map/ppermute | solution.py:29
  404.8 0.9 collective-permute-start.6
  405.8 6.5 %collective-permute-done.6 = f32[16,8,512]{2,1,0:T(8,128)S(1)} collective-permute-done((f32[16,8,512]{2,1,0:T(8,128)S(1)}, f32[16,8,512]{2,1,0:T(8,128)S(1)}, u32[]{:S(2)}, u32[]{:S(2)}) %collective-permute-start.6) | collective-permute-done | bytes 262176 | tf_op jit(solution)/shard_map/ppermute | solution.py:29
  412.4 1.2 collective-permute-done.7
  413.6 1.7 fusion.189
  (28 shorter events, 1.7 us)
Async XLA Ops:
  0.0 34.0 %copy-start.4 = (bf16[5,17]{1,0:T(8,128)(2,1)S(1)}, bf16[5,17]{1,0:T(8,128)(2,1)}, u32[]{:S(2)}) copy-start(bf16[5,17]{1,0:T(8,128)(2,1)} %param.17) | copy-start | bytes 514
  0.0 36.2 %copy-start = (f32[5,17]{1,0:T(8,128)S(1)}, f32[5,17]{1,0:T(8,128)}, u32[]{:S(2)}) copy-start(f32[5,17]{1,0:T(8,128)} %param.15) | copy-start | bytes 1024
  0.0 34.7 %copy-start.1 = (f32[5,17]{1,0:T(8,128)S(1)}, f32[5,17]{1,0:T(8,128)}, u32[]{:S(2)}) copy-start(f32[5,17]{1,0:T(8,128)} %param.16) | copy-start | bytes 1024
  1.1 31.0 %collective-permute-start.1 = (f32[8,16,512]{2,1,0:T(8,128)S(1)}, f32[8,16,512]{2,1,0:T(8,128)S(1)}, u32[]{:S(2)}, u32[]{:S(2)}) collective-permute-start(f32[8,16,512]{2,1,0:T(8,128)S(1)} %get-tuple-element.128), channel_id=1, source_target_pairs={{4,0},{8,4},{12,8},{16,12},{20,16},{24,20},{28,24},{0,28},{5,1},{9... | collective-permute-start | bytes 786440 | tf_op jit(solution)/shard_map/ppermute | solution.py:19
  7.2 23.8 %collective-permute-start = (f32[8,16,512]{2,1,0:T(8,128)S(1)}, f32[8,16,512]{2,1,0:T(8,128)S(1)}, u32[]{:S(2)}, u32[]{:S(2)}) collective-permute-start(f32[8,16,512]{2,1,0:T(8,128)S(1)} %get-tuple-element.129), channel_id=1, source_target_pairs={{0,4},{4,8},{8,12},{12,16},{16,20},{20,24},{24,28},{28,0},{1,5},{5... | collective-permute-start | bytes 786440 | tf_op jit(solution)/shard_map/ppermute | solution.py:17
  32.2 12.5 %collective-permute-start.2 = (f32[32,8,512]{2,1,0:T(8,128)S(1)}, f32[32,8,512]{2,1,0:T(8,128)S(1)}, u32[]{:S(2)}, u32[]{:S(2)}) collective-permute-start(f32[32,8,512]{2,1,0:T(8,128)S(1)} %get-tuple-element.126), channel_id=1, source_target_pairs={{0,1},{1,2},{2,3},{3,0},{4,5},{5,6},{6,7},{7,4},{8,9},{9,10},{10,1... | collective-permute-start | bytes 1572872 | tf_op jit(solution)/shard_map/ppermute | solution.py:17
  32.3 13.2 %collective-permute-start.3 = (f32[32,8,512]{2,1,0:T(8,128)S(1)}, f32[32,8,512]{2,1,0:T(8,128)S(1)}, u32[]{:S(2)}, u32[]{:S(2)}) collective-permute-start(f32[32,8,512]{2,1,0:T(8,128)S(1)} %get-tuple-element.127), channel_id=1, source_target_pairs={{1,0},{2,1},{3,2},{0,3},{5,4},{6,5},{7,6},{4,7},{9,8},{10,9},{11,1... | collective-permute-start | bytes 1572872 | tf_op jit(solution)/shard_map/ppermute | solution.py:19
  287.5 1.5 copy-start.2
  378.6 25.9 %collective-permute-start.4 = (f32[8,32,512]{2,1,0:T(8,128)S(1)}, f32[8,32,512]{2,1,0:T(8,128)S(1)}, u32[]{:S(2)}, u32[]{:S(2)}) collective-permute-start(f32[8,32,512]{2,1,0:T(8,128)S(1)} %get-tuple-element.123), channel_id=1, source_target_pairs={{4,0},{8,4},{12,8},{16,12},{20,16},{24,20},{28,24},{0,28},{5,1},{9... | collective-permute-start | bytes 1572872 | tf_op jit(solution)/shard_map/ppermute | solution.py:29
  383.4 21.2 %collective-permute-start.5 = (f32[8,32,512]{2,1,0:T(8,128)S(1)}, f32[8,32,512]{2,1,0:T(8,128)S(1)}, u32[]{:S(2)}, u32[]{:S(2)}) collective-permute-start(f32[8,32,512]{2,1,0:T(8,128)S(1)} %get-tuple-element.122), channel_id=1, source_target_pairs={{28,0},{0,4},{4,8},{8,12},{12,16},{16,20},{20,24},{24,28},{29,1},{... | collective-permute-start | bytes 1572872 | tf_op jit(solution)/shard_map/ppermute | solution.py:29
  404.8 7.5 %collective-permute-start.6 = (f32[16,8,512]{2,1,0:T(8,128)S(1)}, f32[16,8,512]{2,1,0:T(8,128)S(1)}, u32[]{:S(2)}, u32[]{:S(2)}) collective-permute-start(f32[16,8,512]{2,1,0:T(8,128)S(1)} %get-tuple-element.125), channel_id=1, source_target_pairs={{1,0},{2,1},{3,2},{0,3},{5,4},{6,5},{7,6},{4,7},{9,8},{10,9},{11,1... | collective-permute-start | bytes 786440 | tf_op jit(solution)/shard_map/ppermute | solution.py:29
  405.7 7.8 %collective-permute-start.7 = (f32[16,8,512]{2,1,0:T(8,128)S(1)}, f32[16,8,512]{2,1,0:T(8,128)S(1)}, u32[]{:S(2)}, u32[]{:S(2)}) collective-permute-start(f32[16,8,512]{2,1,0:T(8,128)S(1)} %get-tuple-element.124), channel_id=1, source_target_pairs={{3,0},{0,1},{1,2},{2,3},{7,4},{4,5},{5,6},{6,7},{11,8},{8,9},{9,10... | collective-permute-start | bytes 786440 | tf_op jit(solution)/shard_map/ppermute | solution.py:29
  412.3 1.2 copy-start.3
where the time goes:
time: 419 us; the launch traced here: 415 us
  matrix products  177 us (42%)
  other arithmetic  156 us (37%)
  waiting for transfers between devices  36.7 us (9%)
  local copies, waits for them, and re-layouts  31.4 us (7%)
  starting transfers between devices  13.6 us (3%)
    dot_general x5, matrix products, per_device(): jnp.dot(lowered, bands[density].T, preferred_element_type=jnp.float32)  113 us
    add x5, other arithmetic, per_device(): along_rows + kernel_rows[density, shift_tap] * extended[shift_tap:shift_t...  64.4 us
    dot_general x5, matrix products, per_device(): flat = jnp.dot(lowered, bands[density], preferred_element_type=jnp.float32)  63.9 us
    mul x2, other arithmetic, per_device(): col_weights[:, shift_tap] * spread_rows  44.6 us
    reduce_sum x1, other arithmetic, per_device(): spread = jnp.sum(spread_both, 0)  29.1 us
    ppermute x4, waiting for transfers between devices, from_behind(): return lax.ppermute(block, axis, route)  28.7 us
    mul x1, other arithmetic, per_device(): row_weights[:, shift_tap] * stacked  15.8 us
    slice x5, local copies, waits for them, and re-layouts, per_device(): kernel_rows[density, shift_tap] * extended[shift_tap:shift_tap + span_rows]  8.78 us
  transfers between devices with their start and end apart: 8, of which 5 were waited for; matrix products, arithmetic and copies ran while one was open for 7% of the time, Pallas kernels for 0%

commit v1 on v0

v1 whole, which is shorter than its diff:
```python
import jax
import jax.numpy as jnp
from jax import lax
from jax.experimental import pallas as pl
from jax.experimental.pallas import tpu as pltpu
from jax.sharding import PartitionSpec as P

RADIUS = 8
DENSITIES = 5
TAPS = 2 * RADIUS + 1
LANES = 128


def padded(cells, sides, width):
    for axis, dim in sides:
        count = lax.axis_size(axis)
        head = lax.slice_in_dim(cells, 0, width, axis=dim)
        tail = lax.slice_in_dim(cells, cells.shape[dim] - width, cells.shape[dim], axis=dim)
        cells = jnp.concatenate(
            [
                lax.ppermute(tail, axis, [(i, (i + 1) % count) for i in range(count)]),
                cells,
                lax.ppermute(head, axis, [((i + 1) % count, i) for i in range(count)]),
            ],
            axis=dim,
        )
    return cells


def from_behind(block, axis, distance):
    devices = range(lax.axis_size(axis))
    route = [((i - distance) % len(devices), i) for i in devices]
    return lax.ppermute(block, axis, route)


def split(value):
    high = value.astype(jnp.bfloat16)
    low = (value - high.astype(jnp.float32)).astype(jnp.bfloat16)
    return high, low


def dot(left, right):
    return jnp.dot(left, right, preferred_element_type=jnp.float32)


def picked(taps, index):
    total = jnp.zeros(index.shape, jnp.float32)
    for tap in range(TAPS):
        weight = jnp.broadcast_to(taps[:, tap : tap + 1], index.shape)
        total = jnp.where(index == tap, weight, total)
    return total


def build_forward(sizes, rows, cols, by_row, by_col, high_ref, low_ref):
    span_rows, span_cols, ext_rows, ext_cols = sizes
    wide = ext_rows * ext_cols
    lane = lax.broadcasted_iota(jnp.int32, (span_rows, wide), 1)
    row_index = lane // ext_cols - lax.broadcasted_iota(jnp.int32, (span_rows, wide), 0)
    lane = lax.broadcasted_iota(jnp.int32, (span_cols, wide), 1)
    col_index = lane % ext_cols - lax.broadcasted_iota(jnp.int32, (span_cols, wide), 0)
    for a in range(DENSITIES):
        by_row[...] = picked(rows[a : a + 1], row_index)
        by_col[...] = picked(cols[a : a + 1], col_index)

        def body(r, carry):
            high, low = split(by_row[pl.ds(r, 1), :] * by_col[...])
            start = pl.multiple_of((a * span_rows + r) * span_cols, span_cols)
            high_ref[pl.ds(start, span_cols), :] = high
            low_ref[pl.ds(start, span_cols), :] = low
            return carry

        lax.fori_loop(0, span_rows, body, 0)


def build_backward(sizes, rows, cols, by_row, by_col, high_ref, low_ref):
    span_rows, span_cols, ext_rows, ext_cols = sizes
    own = span_rows * span_cols
    lane = lax.broadcasted_iota(jnp.int32, (ext_rows, own), 1)
    row_index = lax.broadcasted_iota(jnp.int32, (ext_rows, own), 0) - lane // span_cols
    lane = lax.broadcasted_iota(jnp.int32, (ext_cols, own), 1)
    col_index = lax.broadcasted_iota(jnp.int32, (ext_cols, own), 0) - lane % span_cols
    for a in range(DENSITIES):
        by_row[:, a * own : (a + 1) * own] = picked(rows[a : a + 1], row_index)
        by_col[:, a * own : (a + 1) * own] = picked(cols[a : a + 1], col_index)

    def body(r, carry):
        high, low = split(by_row[pl.ds(r, 1), :] * by_col[...])
        start = pl.multiple_of(r * ext_cols, ext_cols)
        high_ref[pl.ds(start, ext_cols), :] = high
        low_ref[pl.ds(start, ext_cols), :] = low
        return carry

    lax.fori_loop(0, ext_rows, body, 0)


def build_bands(depth_taps, band_ref):
    depth = band_ref.shape[1]
    blocks = depth // LANES
    shape = (LANES, LANES)
    index = lax.broadcasted_iota(jnp.int32, shape, 0) - lax.broadcasted_iota(jnp.int32, shape, 1) + RADIUS
    for a in range(DENSITIES):
        taps = depth_taps[a : a + 1]
        same = picked(taps, index).astype(jnp.bfloat16)
        after = picked(taps, index - LANES).astype(jnp.bfloat16)
        before = picked(taps, index + LANES).astype(jnp.bfloat16)
        for p in range(blocks):
            for q in range(blocks):
                block = {0: same, 1: after, -1: before}.get(q - p, jnp.zeros(shape, jnp.bfloat16))
                band_ref[a, p * LANES : (p + 1) * LANES, q * LANES : (q + 1) * LANES] = block


def compute(sizes, ext_ref, hess_ref, rows_ref, cols_ref, depth_ref, out_ref,
            by_row, by_col, by_row_t, by_col_t, fwd_high, fwd_low, bwd_high, bwd_low, bands,
            hess, low_lat, dens, back_high, back_low, hess_sem):
    fetch = pltpu.make_async_copy(hess_ref, hess, hess_sem)
    fetch.start()
    own = sizes[0] * sizes[1]
    rows, cols = rows_ref[...], cols_ref[...]
    build_forward(sizes, rows, cols, by_row, by_col, fwd_high, fwd_low)
    build_backward(sizes, rows, cols, by_row_t, by_col_t, bwd_high, bwd_low)
    build_bands(depth_ref[...].astype(jnp.float32), bands)
    high, low = split(ext_ref[...])

    def lateral(a, carry):
        part = pl.ds(pl.multiple_of(a * own, own), own)
        left = fwd_high[part, :]
        flat = dot(left, high) + dot(left, low) + dot(fwd_low[part, :], high)
        dens[a] = dot(flat.astype(jnp.bfloat16), bands[a])
        return carry

    lax.fori_loop(0, DENSITIES, lateral, 0)
    fetch.wait()

    def gradient(a, carry):
        part = pl.ds(pl.multiple_of(a * own, own), own)
        step = 16
        def piece(i, inner):
            at = pl.ds(pl.multiple_of(i * step, step), step)
            total = hess[a, 0, at, :].astype(jnp.float32) * dens[0, at, :]
            for b in range(1, DENSITIES):
                total = total + hess[a, b, at, :].astype(jnp.float32) * dens[b, at, :]
            low_lat[at, :] = total.astype(jnp.bfloat16)
            return inner
        lax.fori_loop(0, own // step, piece, 0)
        back = lax.dot_general(low_lat[...], bands[a], (((1,), (1,)), ((), ())),
                               preferred_element_type=jnp.float32)
        back_high[part, :], back_low[part, :] = split(back)
        return carry

    lax.fori_loop(0, DENSITIES, gradient, 0)

    tile = 256
    def spread(i, carry):
        at = pl.ds(pl.multiple_of(i * tile, tile), tile)
        left = bwd_high[at, :]
        out_ref[at, :] = (dot(left, back_high[...]) + dot(left, back_low[...])
                          + dot(bwd_low[at, :], back_high[...]))
        return carry
    lax.fori_loop(0, sizes[2] * sizes[3] // tile, spread, 0)


def per_device(tangent, hessian, kernel_rows, kernel_cols, kernel_depth):
    span_rows, span_cols, depth = tangent.shape
    reach = RADIUS
    ext_rows, ext_cols = span_rows + 2 * reach, span_cols + 2 * reach
    sizes = (span_rows, span_cols, ext_rows, ext_cols)
    own, wide = span_rows * span_cols, ext_rows * ext_cols
    extended = padded(tangent, (("gx", 0), ("gy", 1)), RADIUS).reshape(wide, depth)
    full = pl.BlockSpec(memory_space=pltpu.VMEM)
    bf16, f32 = jnp.bfloat16, jnp.float32
    spread = pl.pallas_call(
        lambda *refs: compute(sizes, *refs),
        out_shape=jax.ShapeDtypeStruct((wide, depth), f32),
        in_specs=[full, pl.BlockSpec(memory_space=pl.ANY), full, full, full],
        out_specs=full,
        scratch_shapes=[
            pltpu.VMEM((span_rows, wide), f32),
            pltpu.VMEM((span_cols, wide), f32),
            pltpu.VMEM((ext_rows, DENSITIES * own), f32),
            pltpu.VMEM((ext_cols, DENSITIES * own), f32),
            pltpu.VMEM((DENSITIES * own, wide), bf16),
            pltpu.VMEM((DENSITIES * own, wide), bf16),
            pltpu.VMEM((wide, DENSITIES * own), bf16),
            pltpu.VMEM((wide, DENSITIES * own), bf16),
            pltpu.VMEM((DENSITIES, depth, depth), bf16),
            pltpu.VMEM((DENSITIES, DENSITIES, own, depth), bf16),
            pltpu.VMEM((own, depth), bf16),
            pltpu.VMEM((DENSITIES, own, depth), f32),
            pltpu.VMEM((DENSITIES * own, depth), bf16),
            pltpu.VMEM((DENSITIES * own, depth), bf16),
            pltpu.SemaphoreType.DMA(()),
        ],
        compiler_params=pltpu.CompilerParams(vmem_limit_bytes=56 << 20),
    )(extended, hessian.reshape(DENSITIES, DENSITIES, own, depth), kernel_rows, kernel_cols, kernel_depth)
    spread = spread.reshape(ext_rows, ext_cols, depth)
    middle = spread[reach : reach + span_rows]
    from_next = from_behind(spread[:reach], "gx", -1)
    from_prev = from_behind(spread[span_rows + reach :], "gx", 1)
    middle = middle.at[span_rows - reach :].add(from_next)
    middle = middle.at[:reach].add(from_prev)
    center = middle[:, reach : reach + span_cols]
    from_right = from_behind(middle[:, :reach], "gy", -1)
    from_left = from_behind(middle[:, span_cols + reach :], "gy", 1)
    center = center.at[:, span_cols - reach :].add(from_right)
    center = center.at[:, :reach].add(from_left)
    return center


def solution(mesh):
    return jax.shard_map(
        per_device,
        mesh=mesh,
        in_specs=(P("gx", "gy", None), P(None, None, "gx", "gy", None), P(), P(), P()),
        out_specs=P("gx", "gy", None),
        check_vma=False,
    )
```

time: 419 us -> 94.1 us (0.22)
  matrix products: 177 us -> 0 us
  other arithmetic: 156 us -> 3.51 us
  local copies, waits for them, and re-layouts: 31.4 us -> 3.9 us
  Pallas kernels: 0 us -> 22.8 us
  waiting for transfers between devices: 36.7 us -> 49.8 us
    dot_general x10 -> x0, matrix products: 177 us -> none  [the longest x5 113 us: per_device(): jnp.dot(lowered, bands[density].T, preferred_element_type=jnp.float32)]
    add x5 -> x0, other arithmetic: 64.4 us -> none  [per_device(): along_rows + kernel_rows[density, shift_tap] * extended[shift_tap:shift_t...]
    mul x3 -> x0, other arithmetic: 60.4 us -> none  [the longest x2 44.6 us: per_device(): col_weights[:, shift_tap] * spread_rows]
    reduce_sum x1 -> x0, other arithmetic: 29.1 us -> none  [per_device(): spread = jnp.sum(spread_both, 0)]
    slice x17 -> x0, local copies, waits for them, and re-layouts: 27.4 us -> none  [the longest x5 8.78 us: per_device(): kernel_rows[density, shift_tap] * extended[shift_tap:shift_tap + span_rows]]
    pallas_call x0 -> x1, Pallas kernels: none -> 22.8 us  [per_device(): pl.pallas_call(lambda *refs: compute(sizes, *refs), out_shape=jax.ShapeDt...]
    ppermute x2, waiting for transfers between devices: 7.06 us -> 18.7 us  [padded(): lax.ppermute(tail, axis, [(i, (i + 1) % count) for i in range(count)])]
  transfers between devices with their start and end apart: 8 -> 8, of which waited for: 5 -> 7; matrix products, arithmetic and copies ran while one was open for 7% -> 1% of each run, Pallas kernels for 0% -> 0%
where the time goes in v1:
time: 94.1 us; the launch traced here: 93.5 us
  waiting for transfers between devices  49.8 us (53%)
  Pallas kernels  22.8 us (24%)
  starting transfers between devices  13.4 us (14%)
  local copies, waits for them, and re-layouts  3.9 us (4%)
  other arithmetic  3.51 us (4%)
    ppermute x4, waiting for transfers between devices, from_behind(): return lax.ppermute(block, axis, route)  29.1 us
    pallas_call x1, Pallas kernels, per_device(): pl.pallas_call(lambda *refs: compute(sizes, *refs), out_shape=jax.ShapeDt...  22.8 us
    ppermute x2, waiting for transfers between devices, padded(): lax.ppermute(tail, axis, [(i, (i + 1) % count) for i in range(count)])  18.7 us
    ppermute x4, starting transfers between devices, from_behind(): return lax.ppermute(block, axis, route)  5.48 us
    ppermute x2, starting transfers between devices, padded(): lax.ppermute(head, axis, [((i + 1) % count, i) for i in range(count)])  4.84 us
    ppermute x2, starting transfers between devices, padded(): lax.ppermute(tail, axis, [(i, (i + 1) % count) for i in range(count)])  3.08 us
    ppermute x2, waiting for transfers between devices, padded(): lax.ppermute(head, axis, [((i + 1) % count, i) for i in range(count)])  1.95 us
  transfers between devices with their start and end apart: 8, of which 7 were waited for; matrix products, arithmetic and copies ran while one was open for 1% of the time, Pallas kernels for 0%

profile of v1, /device:TPU:0, one launch (start us, length us, event | category | flops | bytes accessed | tf_op | source)
XLA Modules:
  0.0 93.5 jit_solution(2651905213429865799)
XLA Ops:
  0.0 1.1 %fusion.6 = (f32[8,16,512]{2,1,0:T(8,128)S(1)}, f32[8,16,512]{2,1,0:T(8,128)S(1)}) fusion(f32[16,16,512]{2,1,0:T(8,128)} %param.13), kind=kLoop, calls=%fused_computation.14 | loop fusion | bytes 1048576 | tf_op jit(solution)/shard_map/slice | solution.py:17
  1.1 3.0 %collective-permute-start = (f32[8,16,512]{2,1,0:T(8,128)S(1)}, f32[8,16,512]{2,1,0:T(8,128)S(1)}, u32[]{:S(2)}, u32[]{:S(2)}) collective-permute-start(f32[8,16,512]{2,1,0:T(8,128)S(1)} %get-tuple-element.61), channel_id=1, source_target_pairs={{0,4},{4,8},{8,12},{12,16},{16,20},{20,24},{24,28},{28,0},{1,5},{5... | collective-permute-start | bytes 786440 | tf_op jit(solution)/shard_map/ppermute | solution.py:21
  4.1 3.1 %collective-permute-start.1 = (f32[8,16,512]{2,1,0:T(8,128)S(1)}, f32[8,16,512]{2,1,0:T(8,128)S(1)}, u32[]{:S(2)}, u32[]{:S(2)}) collective-permute-start(f32[8,16,512]{2,1,0:T(8,128)S(1)} %get-tuple-element.60), channel_id=1, source_target_pairs={{4,0},{8,4},{12,8},{16,12},{20,16},{24,20},{28,24},{0,28},{5,1},{9... | collective-permute-start | bytes 786440 | tf_op jit(solution)/shard_map/ppermute | solution.py:23
  7.2 8.1 %collective-permute-done = f32[8,16,512]{2,1,0:T(8,128)S(1)} collective-permute-done((f32[8,16,512]{2,1,0:T(8,128)S(1)}, f32[8,16,512]{2,1,0:T(8,128)S(1)}, u32[]{:S(2)}, u32[]{:S(2)}) %collective-permute-start) | collective-permute-done | bytes 262176 | tf_op jit(solution)/shard_map/ppermute | solution.py:21
  15.3 1.1 %constant_dynamic-update-slice_fusion.1 = f32[32,16,512]{2,1,0:T(8,128)S(1)} fusion(f32[32,16,512]{2,1,0:T(8,128)S(1)} %constant_dynamic-update-slice_fusion.2, f32[16,16,512]{2,1,0:T(8,128)} %param.13), kind=kLoop, calls=%fused_computation.9 | loop fusion | bytes 1048576
  16.4 1.1 %collective-permute-done.1 = f32[8,16,512]{2,1,0:T(8,128)S(1)} collective-permute-done((f32[8,16,512]{2,1,0:T(8,128)S(1)}, f32[8,16,512]{2,1,0:T(8,128)S(1)}, u32[]{:S(2)}, u32[]{:S(2)}) %collective-permute-start.1) | collective-permute-done | bytes 262176 | tf_op jit(solution)/shard_map/ppermute | solution.py:23
  17.5 0.1 fusion.5
  17.6 0.1 collective-permute-start.2
  17.6 1.7 %collective-permute-start.3 = (f32[32,8,512]{2,1,0:T(8,128)S(1)}, f32[32,8,512]{2,1,0:T(8,128)S(1)}, u32[]{:S(2)}, u32[]{:S(2)}) collective-permute-start(f32[32,8,512]{2,1,0:T(8,128)S(1)} %get-tuple-element.59), channel_id=1, source_target_pairs={{1,0},{2,1},{3,2},{0,3},{5,4},{6,5},{7,6},{4,7},{9,8},{10,9},{11,1... | collective-permute-start | bytes 1572872 | tf_op jit(solution)/shard_map/ppermute | solution.py:23
  19.4 10.7 %collective-permute-done.2 = f32[32,8,512]{2,1,0:T(8,128)S(1)} collective-permute-done((f32[32,8,512]{2,1,0:T(8,128)S(1)}, f32[32,8,512]{2,1,0:T(8,128)S(1)}, u32[]{:S(2)}, u32[]{:S(2)}) %collective-permute-start.2) | collective-permute-done | bytes 524320 | tf_op jit(solution)/shard_map/ppermute | solution.py:21
  30.0 0.9 collective-permute-done.3
  30.9 1.6 %pad_maximum_fusion = f32[32,32,512]{2,1,0:T(8,128)} fusion(f32[32,8,512]{2,1,0:T(8,128)S(1)} %collective-permute-done.3, f32[32,16,512]{2,1,0:T(8,128)S(1)} %constant_dynamic-update-slice_fusion, f32[32,8,512]{2,1,0:T(8,128)S(1)} %collective-permute-done.2), kind=kLoop, calls=%fused_computation | loop fusion | flops 1048576 | bytes 4194304 | tf_op jit(solution)/shard_map/concatenate | solution.py:19
  32.4 22.8 %shard_map.55 = f32[1024,512]{1,0:T(8,128)} custom-call(f32[1024,512]{1,0:T(8,128)} %bitcast.7, bf16[5,5,256,512]{3,2,1,0:T(8,128)(2,1)} %bitcast.8, f32[5,17]{1,0:T(8,128)} %refs_2_.1, f32[5,17]{1,0:T(8,128)} %refs_3_.1, bf16[5,17]{1,0:T(8,128)(2,1)} %refs_4_.1), custom_call_target="tpu_custom_call" | custom-call | tf_op jit(solution)/shard_map/pallas_call | solution.py:171
  55.2 0.0 slice-start
  55.3 1.6 %fusion.3 = (f32[256,512]{1,0:T(8,128)S(1)}, f32[256,512]{1,0:T(8,128)S(1)}, f32[256,512]{1,0:T(8,128)S(1)}) fusion(f32[1024,512]{1,0:T(8,128)} %shard_map.55), kind=kLoop, calls=%fused_computation.11 | loop fusion | bytes 3145728 | tf_op jit(solution)/shard_map/slice | solution.py:198
  56.8 4.5 %collective-permute-start.4 = (f32[8,32,512]{2,1,0:T(8,128)S(1)}, f32[8,32,512]{2,1,0:T(8,128)S(1)}, u32[]{:S(2)}, u32[]{:S(2)}) collective-permute-start(f32[8,32,512]{2,1,0:T(8,128)S(1)} %bitcast.11), channel_id=1, source_target_pairs={{4,0},{8,4},{12,8},{16,12},{20,16},{24,20},{28,24},{0,28},{5,1},{9... | collective-permute-start | bytes 1572872 | tf_op jit(solution)/shard_map/ppermute | solution.py:33
  61.3 0.0 collective-permute-start.5
  61.3 21.4 %collective-permute-done.4 = f32[8,32,512]{2,1,0:T(8,128)S(1)} collective-permute-done((f32[8,32,512]{2,1,0:T(8,128)S(1)}, f32[8,32,512]{2,1,0:T(8,128)S(1)}, u32[]{:S(2)}, u32[]{:S(2)}) %collective-permute-start.4) | collective-permute-done | bytes 524320 | tf_op jit(solution)/shard_map/ppermute | solution.py:33
  82.7 0.0 slice-done
  82.7 0.1 add_dynamic-update-slice_fusion
  82.8 0.0 collective-permute-done.5
  82.8 0.1 fusion
  83.0 1.0 %collective-permute-start.6 = (f32[16,8,512]{2,1,0:T(8,128)S(1)}, f32[16,8,512]{2,1,0:T(8,128)S(1)}, u32[]{:S(2)}, u32[]{:S(2)}) collective-permute-start(f32[16,8,512]{2,1,0:T(8,128)S(1)} %get-tuple-element.57), channel_id=1, source_target_pairs={{1,0},{2,1},{3,2},{0,3},{5,4},{6,5},{7,6},{4,7},{9,8},{10,9},{11,1... | collective-permute-start | bytes 786440 | tf_op jit(solution)/shard_map/ppermute | solution.py:33
  84.0 0.0 collective-permute-start.7
  84.0 6.6 %collective-permute-done.6 = f32[16,8,512]{2,1,0:T(8,128)S(1)} collective-permute-done((f32[16,8,512]{2,1,0:T(8,128)S(1)}, f32[16,8,512]{2,1,0:T(8,128)S(1)}, u32[]{:S(2)}, u32[]{:S(2)}) %collective-permute-start.6) | collective-permute-done | bytes 262176 | tf_op jit(solution)/shard_map/ppermute | solution.py:33
  90.6 0.0 copy-start
  90.7 1.1 %collective-permute-done.7 = f32[16,8,512]{2,1,0:T(8,128)S(1)} collective-permute-done((f32[16,8,512]{2,1,0:T(8,128)S(1)}, f32[16,8,512]{2,1,0:T(8,128)S(1)}, u32[]{:S(2)}, u32[]{:S(2)}) %collective-permute-start.7) | collective-permute-done | bytes 262176 | tf_op jit(solution)/shard_map/ppermute | solution.py:33
  91.8 0.0 copy-done
  91.8 1.7 %fusion.1 = f32[16,16,512]{2,1,0:T(8,128)} fusion(f32[16,16,512]{2,1,0:T(8,128)} %copy-done, f32[16,8,512]{2,1,0:T(8,128)S(1)} %collective-permute-done.7), kind=kLoop, calls=%fused_computation.5 | loop fusion | flops 65536 | bytes 786432 | tf_op jit(solution)/shard_map/scatter-add | solution.py:205
  (5 shorter events, 0.1 us)
Async XLA Ops:
  1.1 14.2 %collective-permute-start = (f32[8,16,512]{2,1,0:T(8,128)S(1)}, f32[8,16,512]{2,1,0:T(8,128)S(1)}, u32[]{:S(2)}, u32[]{:S(2)}) collective-permute-start(f32[8,16,512]{2,1,0:T(8,128)S(1)} %get-tuple-element.61), channel_id=1, source_target_pairs={{0,4},{4,8},{8,12},{12,16},{16,20},{20,24},{24,28},{28,0},{1,5},{5... | collective-permute-start | bytes 786440 | tf_op jit(solution)/shard_map/ppermute | solution.py:21
  4.1 13.4 %collective-permute-start.1 = (f32[8,16,512]{2,1,0:T(8,128)S(1)}, f32[8,16,512]{2,1,0:T(8,128)S(1)}, u32[]{:S(2)}, u32[]{:S(2)}) collective-permute-start(f32[8,16,512]{2,1,0:T(8,128)S(1)} %get-tuple-element.60), channel_id=1, source_target_pairs={{4,0},{8,4},{12,8},{16,12},{20,16},{24,20},{28,24},{0,28},{5,1},{9... | collective-permute-start | bytes 786440 | tf_op jit(solution)/shard_map/ppermute | solution.py:23
  17.6 12.5 %collective-permute-start.2 = (f32[32,8,512]{2,1,0:T(8,128)S(1)}, f32[32,8,512]{2,1,0:T(8,128)S(1)}, u32[]{:S(2)}, u32[]{:S(2)}) collective-permute-start(f32[32,8,512]{2,1,0:T(8,128)S(1)} %get-tuple-element.58), channel_id=1, source_target_pairs={{0,1},{1,2},{2,3},{3,0},{4,5},{5,6},{6,7},{7,4},{8,9},{9,10},{10,1... | collective-permute-start | bytes 1572872 | tf_op jit(solution)/shard_map/ppermute | solution.py:21
  17.6 13.2 %collective-permute-start.3 = (f32[32,8,512]{2,1,0:T(8,128)S(1)}, f32[32,8,512]{2,1,0:T(8,128)S(1)}, u32[]{:S(2)}, u32[]{:S(2)}) collective-permute-start(f32[32,8,512]{2,1,0:T(8,128)S(1)} %get-tuple-element.59), channel_id=1, source_target_pairs={{1,0},{2,1},{3,2},{0,3},{5,4},{6,5},{7,6},{4,7},{9,8},{10,9},{11,1... | collective-permute-start | bytes 1572872 | tf_op jit(solution)/shard_map/ppermute | solution.py:23
  55.2 27.5 %slice-start = ((f32[1024,512]{1,0:T(8,128)}), f32[512,512]{1,0:T(8,128)S(1)}, s32[]{:S(2)}) async-start(f32[1024,512]{1,0:T(8,128)} %shard_map.55), calls=%async_computation | async-start | bytes 2097152 | tf_op jit(solution)/shard_map/slice | solution.py:196
  56.8 25.9 %collective-permute-start.4 = (f32[8,32,512]{2,1,0:T(8,128)S(1)}, f32[8,32,512]{2,1,0:T(8,128)S(1)}, u32[]{:S(2)}, u32[]{:S(2)}) collective-permute-start(f32[8,32,512]{2,1,0:T(8,128)S(1)} %bitcast.11), channel_id=1, source_target_pairs={{4,0},{8,4},{12,8},{16,12},{20,16},{24,20},{28,24},{0,28},{5,1},{9... | collective-permute-start | bytes 1572872 | tf_op jit(solution)/shard_map/ppermute | solution.py:33
  61.3 21.5 %collective-permute-start.5 = (f32[8,32,512]{2,1,0:T(8,128)S(1)}, f32[8,32,512]{2,1,0:T(8,128)S(1)}, u32[]{:S(2)}, u32[]{:S(2)}) collective-permute-start(f32[8,32,512]{2,1,0:T(8,128)S(1)} %bitcast.10), channel_id=1, source_target_pairs={{28,0},{0,4},{4,8},{8,12},{12,16},{16,20},{20,24},{24,28},{29,1},{... | collective-permute-start | bytes 1572872 | tf_op jit(solution)/shard_map/ppermute | solution.py:33
  83.0 7.6 %collective-permute-start.6 = (f32[16,8,512]{2,1,0:T(8,128)S(1)}, f32[16,8,512]{2,1,0:T(8,128)S(1)}, u32[]{:S(2)}, u32[]{:S(2)}) collective-permute-start(f32[16,8,512]{2,1,0:T(8,128)S(1)} %get-tuple-element.57), channel_id=1, source_target_pairs={{1,0},{2,1},{3,2},{0,3},{5,4},{6,5},{7,6},{4,7},{9,8},{10,9},{11,1... | collective-permute-start | bytes 786440 | tf_op jit(solution)/shard_map/ppermute | solution.py:33
  84.0 7.8 %collective-permute-start.7 = (f32[16,8,512]{2,1,0:T(8,128)S(1)}, f32[16,8,512]{2,1,0:T(8,128)S(1)}, u32[]{:S(2)}, u32[]{:S(2)}) collective-permute-start(f32[16,8,512]{2,1,0:T(8,128)S(1)} %get-tuple-element.56), channel_id=1, source_target_pairs={{3,0},{0,1},{1,2},{2,3},{7,4},{4,5},{5,6},{6,7},{11,8},{8,9},{9,10... | collective-permute-start | bytes 786440 | tf_op jit(solution)/shard_map/ppermute | solution.py:33
  90.6 1.1 %copy-start = (f32[16,16,512]{2,1,0:T(8,128)}, f32[16,16,512]{2,1,0:T(8,128)S(1)}, u32[]{:S(2)}) copy-start(f32[16,16,512]{2,1,0:T(8,128)S(1)} %fusion.2) | copy-start | bytes 1572868

commit v2 on v1

--- a/solution.py
+++ b/solution.py
@@ -9,28 +9,6 @@
 DENSITIES = 5
 TAPS = 2 * RADIUS + 1
 LANES = 128
-
-
-def padded(cells, sides, width):
-    for axis, dim in sides:
-        count = lax.axis_size(axis)
-        head = lax.slice_in_dim(cells, 0, width, axis=dim)
-        tail = lax.slice_in_dim(cells, cells.shape[dim] - width, cells.shape[dim], axis=dim)
-        cells = jnp.concatenate(
-            [
-                lax.ppermute(tail, axis, [(i, (i + 1) % count) for i in range(count)]),
-                cells,
-                lax.ppermute(head, axis, [((i + 1) % count, i) for i in range(count)]),
-            ],
-            axis=dim,
-        )
-    return cells
-
-
-def from_behind(block, axis, distance):
-    devices = range(lax.axis_size(axis))
-    route = [((i - distance) % len(devices), i) for i in devices]
-    return lax.ppermute(block, axis, route)
 
 
 def split(value):
@@ -109,54 +87,218 @@
                 band_ref[a, p * LANES : (p + 1) * LANES, q * LANES : (q + 1) * LANES] = block
 
 
-def compute(sizes, ext_ref, hess_ref, rows_ref, cols_ref, depth_ref, out_ref,
-            by_row, by_col, by_row_t, by_col_t, fwd_high, fwd_low, bwd_high, bwd_low, bands,
-            hess, low_lat, dens, back_high, back_low, hess_sem):
-    fetch = pltpu.make_async_copy(hess_ref, hess, hess_sem)
+def compute(sizes, counts, tangent_ref, hess_ref, rows_ref, cols_ref, depth_ref, out_ref,
+            ext, high, low, by_row, by_col, by_row_t, by_col_t, fwd_high, fwd_low, bwd_high, bwd_low,
+            bands, hess, lowered, acc, back_high, back_low, spread, from_left, from_right,
+            from_up, from_down, local_sems, send_sems, recv_sems, back_send_sems, back_recv_sems):
+    span_rows, span_cols, ext_rows, ext_cols = sizes
+    depth = acc.shape[1]
+    reach = RADIUS
+    own, wide = span_rows * span_cols, ext_rows * ext_cols
+    gx, gy = lax.axis_index("gx"), lax.axis_index("gy")
+    up = {"gx": lax.rem(gx + counts[0] - 1, counts[0])}
+    down = {"gx": lax.rem(gx + 1, counts[0])}
+    left = {"gy": lax.rem(gy + counts[1] - 1, counts[1])}
+    right = {"gy": lax.rem(gy + 1, counts[1])}
+    mesh_ids = pl.DeviceIdType.MESH
+
+    fetch = pltpu.make_async_copy(hess_ref, hess, local_sems.at[0])
     fetch.start()
-    own = sizes[0] * sizes[1]
+    inner_rows, inner_cols = pl.ds(reach, span_rows), pl.ds(reach, span_cols)
+    home = pltpu.make_async_copy(tangent_ref, ext.at[inner_rows, inner_cols, :], local_sems.at[1])
+    home.start()
+
+    barrier = pltpu.get_barrier_semaphore()
+    for neighbour in (up, down, left, right):
+        pl.semaphore_signal(barrier, inc=1, device_id=neighbour, device_id_type=mesh_ids)
+    pl.semaphore_wait(barrier, 4)
+
+    first, last = pl.ds(0, reach), pl.ds(reach + span_rows, reach)
+    first_cols, last_cols = pl.ds(0, reach), pl.ds(reach + span_cols, reach)
+    chunks = depth // LANES
+    lanes = [pl.ds(c * LANES, LANES) for c in range(chunks)]
+
+    def remote(source, target, send_sem, recv_sem, device):
+        return pltpu.make_async_remote_copy(
+            src_ref=source, dst_ref=target, send_sem=send_sem, recv_sem=recv_sem,
+            device_id=device, device_id_type=mesh_ids)
+
+    head_rows, tail_rows = pl.ds(0, reach), pl.ds(span_rows - reach, reach)
+    head_cols, tail_cols = pl.ds(0, reach), pl.ds(span_cols - reach, reach)
+    copies = {}
+    for c in range(chunks):
+        z = lanes[c]
+        every_row, every_col = pl.ds(0, span_rows), pl.ds(0, span_cols)
+        plan = [
+            (tangent_ref.at[tail_rows, every_col, z], ext.at[first, inner_cols, z], down),
+            (tangent_ref.at[head_rows, every_col, z], ext.at[last, inner_cols, z], up),
+            (tangent_ref.at[every_row, tail_cols, z], ext.at[inner_rows, first_cols, z], right),
+            (tangent_ref.at[every_row, head_cols, z], ext.at[inner_rows, last_cols, z], left),
+        ]
+        near_last, near_first = pl.ds(span_cols, reach), pl.ds(reach, reach)
+        for rows_at in (first, last):
+            plan.append((ext.at[rows_at, near_last, z], ext.at[rows_at, first_cols, z], right))
+            plan.append((ext.at[rows_at, near_first, z], ext.at[rows_at, last_cols, z], left))
+        for kind, (source, target, device) in enumerate(plan):
+            copies[kind, c] = remote(source, target, send_sems.at[kind, c], recv_sems.at[kind, c], device)
+    for c in range(chunks):
+        for kind in range(4):
+            copies[kind, c].start()
+
+    def relay(c):
+        for kind in (0, 1):
+            copies[kind, c].wait_recv()
+        for kind in (4, 5, 6, 7):
+            copies[kind, c].start()
+
     rows, cols = rows_ref[...], cols_ref[...]
     build_forward(sizes, rows, cols, by_row, by_col, fwd_high, fwd_low)
+    home.wait()
+
+    halves = max(1, depth // 256)
+    half = depth // halves
+    per_half = chunks // halves
+    edge = reach * ext_cols
+
+    def prepare(h, start, count):
+        z = pl.ds(h * half, half)
+        block = ext[pl.ds(start, count), :, z].reshape(count * ext_cols, half)
+        at = pl.ds(start * ext_cols, count * ext_cols)
+        high[at, z], low[at, z] = split(block)
+
+    def lateral(h, ranges, fresh):
+        z = pl.ds(h * half, half)
+
+        def body(a, carry):
+            part = pl.ds(pl.multiple_of(a * own, own), own)
+            total = None if fresh else acc[part, z]
+            for start, count in ranges:
+                at = pl.ds(start, count)
+                lead = fwd_high[part, at]
+                piece = (dot(lead, high[at, z]) + dot(lead, low[at, z])
+                         + dot(fwd_low[part, at], high[at, z]))
+                total = piece if total is None else total + piece
+            acc[part, z] = total
+            return carry
+
+        lax.fori_loop(0, DENSITIES, body, 0)
+
+    def middle(h):
+        for c in range(h * per_half, (h + 1) * per_half):
+            copies[2, c].wait_recv()
+            copies[3, c].wait_recv()
+        prepare(h, reach, span_rows)
+        lateral(h, [(edge, span_rows * ext_cols)], True)
+
+    def edges(h):
+        for c in range(h * per_half, (h + 1) * per_half):
+            for kind in (4, 5, 6, 7):
+                copies[kind, c].wait_recv()
+        prepare(h, 0, reach)
+        prepare(h, reach + span_rows, reach)
+        lateral(h, [(0, edge), (edge + span_rows * ext_cols, edge)], False)
+
+    build_bands(depth_ref[...].astype(jnp.float32), bands)
+    relayed = 0
+    for h in range(halves):
+        middle(h)
+        relay(relayed)
+        relayed += 1
     build_backward(sizes, rows, cols, by_row_t, by_col_t, bwd_high, bwd_low)
-    build_bands(depth_ref[...].astype(jnp.float32), bands)
-    high, low = split(ext_ref[...])
-
-    def lateral(a, carry):
+    for h in range(halves):
+        while relayed < min(chunks, (h + 1) * per_half + 1):
+            relay(relayed)
+            relayed += 1
+        edges(h)
+
+    def along_depth(a, carry):
         part = pl.ds(pl.multiple_of(a * own, own), own)
-        left = fwd_high[part, :]
-        flat = dot(left, high) + dot(left, low) + dot(fwd_low[part, :], high)
-        dens[a] = dot(flat.astype(jnp.bfloat16), bands[a])
+        acc[part, :] = dot(acc[part, :].astype(jnp.bfloat16), bands[a])
         return carry
 
-    lax.fori_loop(0, DENSITIES, lateral, 0)
+    lax.fori_loop(0, DENSITIES, along_depth, 0)
     fetch.wait()
 
     def gradient(a, carry):
         part = pl.ds(pl.multiple_of(a * own, own), own)
         step = 16
+
         def piece(i, inner):
             at = pl.ds(pl.multiple_of(i * step, step), step)
-            total = hess[a, 0, at, :].astype(jnp.float32) * dens[0, at, :]
-            for b in range(1, DENSITIES):
-                total = total + hess[a, b, at, :].astype(jnp.float32) * dens[b, at, :]
-            low_lat[at, :] = total.astype(jnp.bfloat16)
+            total = None
+            for b in range(DENSITIES):
+                there = pl.ds(pl.multiple_of(b * own + i * step, step), step)
+                term = hess[a, b, at, :].astype(jnp.float32) * acc[there, :]
+                total = term if total is None else total + term
+            lowered[at, :] = total.astype(jnp.bfloat16)
             return inner
+
         lax.fori_loop(0, own // step, piece, 0)
-        back = lax.dot_general(low_lat[...], bands[a], (((1,), (1,)), ((), ())),
+        back = lax.dot_general(lowered[...], bands[a], (((1,), (1,)), ((), ())),
                                preferred_element_type=jnp.float32)
         back_high[part, :], back_low[part, :] = split(back)
         return carry
 
     lax.fori_loop(0, DENSITIES, gradient, 0)
 
-    tile = 256
-    def spread(i, carry):
-        at = pl.ds(pl.multiple_of(i * tile, tile), tile)
-        left = bwd_high[at, :]
-        out_ref[at, :] = (dot(left, back_high[...]) + dot(left, back_low[...])
-                          + dot(bwd_low[at, :], back_high[...]))
-        return carry
-    lax.fori_loop(0, sizes[2] * sizes[3] // tile, spread, 0)
+    def contribute(h, start, count):
+        z = pl.ds(h * half, half)
+        at = pl.ds(start * ext_cols, count * ext_cols)
+        lead = bwd_high[at, :]
+        flat = dot(lead, back_high[:, z]) + dot(lead, back_low[:, z]) + dot(bwd_low[at, :], back_high[:, z])
+        spread[pl.ds(start, count), :, z] = flat.reshape(count, ext_cols, half)
+
+    returns = {}
+    for h in range(halves):
+        z = pl.ds(h * half, half)
+        plan = []
+        for rows_at in (first, last, inner_rows):
+            plan.append((spread.at[rows_at, last_cols, z], from_left.at[rows_at, :, z], right))
+            plan.append((spread.at[rows_at, first_cols, z], from_right.at[rows_at, :, z], left))
+        plan.append((spread.at[first, inner_cols, z], from_down.at[:, :, z], up))
+        plan.append((spread.at[last, inner_cols, z], from_up.at[:, :, z], down))
+        for kind, (source, target, device) in enumerate(plan):
+            returns[kind, h] = remote(source, target, back_send_sems.at[kind, h], back_recv_sems.at[kind, h], device)
+
+    for h in range(halves):
+        contribute(h, 0, reach)
+        for kind in (0, 1):
+            returns[kind, h].start()
+        contribute(h, reach + span_rows, reach)
+        for kind in (2, 3):
+            returns[kind, h].start()
+
+    def strips(h):
+        z = pl.ds(h * half, half)
+        for kind, rows_at, strip in ((0, first, 6), (2, last, 7)):
+            returns[kind, h].wait_recv()
+            returns[kind + 1, h].wait_recv()
+            near = pl.ds(reach, reach)
+            spread[rows_at, near, z] = spread[rows_at, near, z] + from_left[rows_at, :, z]
+            far = pl.ds(span_cols, reach)
+            spread[rows_at, far, z] = spread[rows_at, far, z] + from_right[rows_at, :, z]
+            returns[strip, h].start()
+
+    for h in range(halves):
+        strips(h)
+    for h in range(halves):
+        for start in range(reach, reach + span_rows, reach):
+            contribute(h, start, reach)
+        for kind in (4, 5):
+            returns[kind, h].start()
+    for h in range(halves):
+        z = pl.ds(h * half, half)
+        for kind in (4, 5):
+            returns[kind, h].wait_recv()
+        out_ref[:, :, z] = spread[inner_rows, inner_cols, z]
+        out_ref[:, head_cols, z] = out_ref[:, head_cols, z] + from_left[inner_rows, :, z]
+        out_ref[:, tail_cols, z] = out_ref[:, tail_cols, z] + from_right[inner_rows, :, z]
+        for kind in (6, 7):
+            returns[kind, h].wait_recv()
+        out_ref[head_rows, :, z] = out_ref[head_rows, :, z] + from_up[:, :, z]
+        out_ref[tail_rows, :, z] = out_ref[tail_rows, :, z] + from_down[:, :, z]
+    for copy in list(copies.values()) + list(returns.values()):
+        copy.wait_send()
 
 
 def per_device(tangent, hessian, kernel_rows, kernel_cols, kernel_depth):
@@ -164,16 +306,21 @@
     reach = RADIUS
     ext_rows, ext_cols = span_rows + 2 * reach, span_cols + 2 * reach
     sizes = (span_rows, span_cols, ext_rows, ext_cols)
+    counts = (lax.axis_size("gx"), lax.axis_size("gy"))
     own, wide = span_rows * span_cols, ext_rows * ext_cols
-    extended = padded(tangent, (("gx", 0), ("gy", 1)), RADIUS).reshape(wide, depth)
+    chunks, halves = depth // LANES, max(1, depth // 256)
     full = pl.BlockSpec(memory_space=pltpu.VMEM)
+    anywhere = pl.BlockSpec(memory_space=pl.ANY)
     bf16, f32 = jnp.bfloat16, jnp.float32
-    spread = pl.pallas_call(
-        lambda *refs: compute(sizes, *refs),
-        out_shape=jax.ShapeDtypeStruct((wide, depth), f32),
-        in_specs=[full, pl.BlockSpec(memory_space=pl.ANY), full, full, full],
+    return pl.pallas_call(
+        lambda *refs: compute(sizes, counts, *refs),
+        out_shape=jax.ShapeDtypeStruct((span_rows, span_cols, depth), f32),
+        in_specs=[anywhere, anywhere, full, full, full],
         out_specs=full,
         scratch_shapes=[
+            pltpu.VMEM((ext_rows, ext_cols, depth), f32),
+            pltpu.VMEM((wide, depth), bf16),
+            pltpu.VMEM((wide, depth), bf16),
             pltpu.VMEM((span_rows, wide), f32),
             pltpu.VMEM((span_cols, wide), f32),
             pltpu.VMEM((ext_rows, DENSITIES * own), f32),
@@ -185,25 +332,23 @@
             pltpu.VMEM((DENSITIES, depth, depth), bf16),
             pltpu.VMEM((DENSITIES, DENSITIES, own, depth), bf16),
             pltpu.VMEM((own, depth), bf16),
-            pltpu.VMEM((DENSITIES, own, depth), f32),
+            pltpu.VMEM((DENSITIES * own, depth), f32),
             pltpu.VMEM((DENSITIES * own, depth), bf16),
             pltpu.VMEM((DENSITIES * own, depth), bf16),
-            pltpu.SemaphoreType.DMA(()),
+            pltpu.VMEM((ext_rows, ext_cols, depth), f32),
+            pltpu.VMEM((ext_rows, reach, depth), f32),
+            pltpu.VMEM((ext_rows, reach, depth), f32),
+            pltpu.VMEM((reach, span_cols, depth), f32),
+            pltpu.VMEM((reach, span_cols, depth), f32),
+            pltpu.SemaphoreType.DMA((2,)),
+            pltpu.SemaphoreType.DMA((8, chunks)),
+            pltpu.SemaphoreType.DMA((8, chunks)),
+            pltpu.SemaphoreType.DMA((8, halves)),
+            pltpu.SemaphoreType.DMA((8, halves)),
         ],
-        compiler_params=pltpu.CompilerParams(vmem_limit_bytes=56 << 20),
-    )(extended, hessian.reshape(DENSITIES, DENSITIES, own, depth), kernel_rows, kernel_cols, kernel_depth)
-    spread = spread.reshape(ext_rows, ext_cols, depth)
-    middle = spread[reach : reach + span_rows]
-    from_next = from_behind(spread[:reach], "gx", -1)
-    from_prev = from_behind(spread[span_rows + reach :], "gx", 1)
-    middle = middle.at[span_rows - reach :].add(from_next)
-    middle = middle.at[:reach].add(from_prev)
-    center = middle[:, reach : reach + span_cols]
-    from_right = from_behind(middle[:, :reach], "gy", -1)
-    from_left = from_behind(middle[:, span_cols + reach :], "gy", 1)
-    center = center.at[:, span_cols - reach :].add(from_right)
-    center = center.at[:, :reach].add(from_left)
-    return center
+        compiler_params=pltpu.CompilerParams(
+            vmem_limit_bytes=60 << 20, collective_id=0, has_side_effects=True),
+    )(tangent, hessian.reshape(DENSITIES, DENSITIES, own, depth), kernel_rows, kernel_cols, kernel_depth)
 
 
 def solution(mesh):

time: 94.1 us -> 53.2 us (0.57)
  waiting for transfers between devices: 49.8 us -> 0 us
  Pallas kernels: 22.8 us -> 51.1 us
  starting transfers between devices: 13.4 us -> 0 us
  other arithmetic: 3.51 us -> 0 us
  local copies, waits for them, and re-layouts: 3.9 us -> 1.88 us
    ppermute x8 -> x0, waiting for transfers between devices: 49.8 us -> none  [the longest x4 29.1 us: from_behind(): return lax.ppermute(block, axis, route)]
    pallas_call x1, Pallas kernels: 22.8 us -> 51.1 us  [per_device(): pl.pallas_call(lambda *refs: compute(sizes, counts, *refs), out_shape=jax...]
    ppermute x8 -> x0, starting transfers between devices: 13.4 us -> none  [the longest x4 5.48 us: from_behind(): return lax.ppermute(block, axis, route)]
    slice x7 -> x0, local copies, waits for them, and re-layouts: 2.78 us -> none  [the longest x1 1.57 us: per_device(): from_prev = from_behind(spread[span_rows + reach:], 'gx', 1)]
    scatter-add x4 -> x0, other arithmetic: 1.96 us -> none  [the longest x1 1.7 us: per_device(): center = center.at[:, :reach].add(from_left)]
    concatenate x1 -> x0, other arithmetic: 1.55 us -> none  [padded(): jnp.concatenate([lax.ppermute(tail, axis, [(i, (i + 1) % count) for i in...]
  transfers between devices with their start and end apart: 8 -> 0, of which waited for: 7 -> 0; matrix products, arithmetic and copies ran while one was open for 1% -> 0% of each run, Pallas kernels for 0% -> 0%
where the time goes in v2:
time: 53.2 us; the launch traced here: 53 us
  Pallas kernels  51.1 us (96%)
  local copies, waits for them, and re-layouts  1.88 us (4%)
    pallas_call x1, Pallas kernels, per_device(): pl.pallas_call(lambda *refs: compute(sizes, counts, *refs), out_shape=jax...  51.1 us
    unnamed x1, local copies, waits for them, and re-layouts  1.88 us

profile of v2, /device:TPU:0, one launch (start us, length us, event | category | flops | bytes accessed | tf_op | source)
XLA Modules:
  0.0 53.0 jit_solution(5153638547529582025)
XLA Ops:
  0.0 51.1 %shard_map.55 = f32[16,16,512]{2,1,0:T(8,128)} custom-call(f32[16,16,512]{2,1,0:T(8,128)} %refs_0_.1, bf16[5,5,256,512]{3,2,1,0:T(8,128)(2,1)} %bitcast.1, f32[5,17]{1,0:T(8,128)} %refs_2_.1, f32[5,17]{1,0:T(8,128)} %refs_3_.1, bf16[5,17]{1,0:T(8,128)(2,1)} %refs_4_.1), custom_call_target="tpu_custom_call" | custom-call | tf_op jit(solution)/shard_map/pallas_call | solution.py:315
  51.1 1.9 %copy.7 = f32[16,16,512]{2,1,0:T(8,128)} copy(f32[16,16,512]{2,1,0:T(8,128)} %shard_map.55) | data formatting | bytes 1048576

commit v3 on v2

--- a/solution.py
+++ b/solution.py
@@ -89,7 +89,7 @@
 
 def compute(sizes, counts, tangent_ref, hess_ref, rows_ref, cols_ref, depth_ref, out_ref,
             ext, high, low, by_row, by_col, by_row_t, by_col_t, fwd_high, fwd_low, bwd_high, bwd_low,
-            bands, hess, lowered, acc, back_high, back_low, spread, from_left, from_right,
+            bands, hess, lowered, acc, dens, back_high, back_low, spread, from_left, from_right,
             from_up, from_down, local_sems, send_sems, recv_sems, back_send_sems, back_recv_sems):
     span_rows, span_cols, ext_rows, ext_cols = sizes
     depth = acc.shape[1]
@@ -111,6 +111,10 @@
     barrier = pltpu.get_barrier_semaphore()
     for neighbour in (up, down, left, right):
         pl.semaphore_signal(barrier, inc=1, device_id=neighbour, device_id_type=mesh_ids)
+    rows, cols = rows_ref[...], cols_ref[...]
+    build_forward(sizes, rows, cols, by_row, by_col, fwd_high, fwd_low)
+    build_bands(depth_ref[...].astype(jnp.float32), bands)
+    build_backward(sizes, rows, cols, by_row_t, by_col_t, bwd_high, bwd_low)
     pl.semaphore_wait(barrier, 4)
 
     first, last = pl.ds(0, reach), pl.ds(reach + span_rows, reach)
@@ -151,8 +155,6 @@
         for kind in (4, 5, 6, 7):
             copies[kind, c].start()
 
-    rows, cols = rows_ref[...], cols_ref[...]
-    build_forward(sizes, rows, cols, by_row, by_col, fwd_high, fwd_low)
     home.wait()
 
     halves = max(1, depth // 256)
@@ -160,15 +162,12 @@
     per_half = chunks // halves
     edge = reach * ext_cols
 
-    def prepare(h, start, count):
-        z = pl.ds(h * half, half)
-        block = ext[pl.ds(start, count), :, z].reshape(count * ext_cols, half)
+    def prepare(z, start, count):
+        block = ext[pl.ds(start, count), :, z].reshape(count * ext_cols, z.size)
         at = pl.ds(start * ext_cols, count * ext_cols)
         high[at, z], low[at, z] = split(block)
 
-    def lateral(h, ranges, fresh):
-        z = pl.ds(h * half, half)
-
+    def lateral(z, ranges, fresh):
         def body(a, carry):
             part = pl.ds(pl.multiple_of(a * own, own), own)
             total = None if fresh else acc[part, z]
@@ -187,59 +186,50 @@
         for c in range(h * per_half, (h + 1) * per_half):
             copies[2, c].wait_recv()
             copies[3, c].wait_recv()
-        prepare(h, reach, span_rows)
-        lateral(h, [(edge, span_rows * ext_cols)], True)
-
-    def edges(h):
-        for c in range(h * per_half, (h + 1) * per_half):
+        z = pl.ds(h * half, half)
+        prepare(z, reach, span_rows)
+        lateral(z, [(edge, span_rows * ext_cols)], True)
+
+    def edges(begin, end):
+        for c in range(begin, end):
             for kind in (4, 5, 6, 7):
                 copies[kind, c].wait_recv()
-        prepare(h, 0, reach)
-        prepare(h, reach + span_rows, reach)
-        lateral(h, [(0, edge), (edge + span_rows * ext_cols, edge)], False)
-
-    build_bands(depth_ref[...].astype(jnp.float32), bands)
-    relayed = 0
-    for h in range(halves):
-        middle(h)
-        relay(relayed)
-        relayed += 1
-    build_backward(sizes, rows, cols, by_row_t, by_col_t, bwd_high, bwd_low)
-    for h in range(halves):
-        while relayed < min(chunks, (h + 1) * per_half + 1):
-            relay(relayed)
-            relayed += 1
-        edges(h)
-
-    def along_depth(a, carry):
-        part = pl.ds(pl.multiple_of(a * own, own), own)
-        acc[part, :] = dot(acc[part, :].astype(jnp.bfloat16), bands[a])
-        return carry
-
-    lax.fori_loop(0, DENSITIES, along_depth, 0)
-    fetch.wait()
-
-    def gradient(a, carry):
-        part = pl.ds(pl.multiple_of(a * own, own), own)
-        step = 16
-
-        def piece(i, inner):
-            at = pl.ds(pl.multiple_of(i * step, step), step)
-            total = None
-            for b in range(DENSITIES):
-                there = pl.ds(pl.multiple_of(b * own + i * step, step), step)
-                term = hess[a, b, at, :].astype(jnp.float32) * acc[there, :]
-                total = term if total is None else total + term
-            lowered[at, :] = total.astype(jnp.bfloat16)
-            return inner
-
-        lax.fori_loop(0, own // step, piece, 0)
-        back = lax.dot_general(lowered[...], bands[a], (((1,), (1,)), ((), ())),
-                               preferred_element_type=jnp.float32)
-        back_high[part, :], back_low[part, :] = split(back)
-        return carry
-
-    lax.fori_loop(0, DENSITIES, gradient, 0)
+        z = pl.ds(begin * LANES, (end - begin) * LANES)
+        prepare(z, 0, reach)
+        prepare(z, reach + span_rows, reach)
+        lateral(z, [(0, edge), (edge + span_rows * ext_cols, edge)], False)
+
+    def along_depth(source, target):
+        def body(a, carry):
+            part = pl.ds(pl.multiple_of(a * own, own), own)
+            dens[part, target] = dot(acc[part, source].astype(jnp.bfloat16), bands[a, source, target])
+            return carry
+
+        lax.fori_loop(0, DENSITIES, body, 0)
+
+    def gradient(middle_lanes, source, target):
+        def body(a, carry):
+            part = pl.ds(pl.multiple_of(a * own, own), own)
+            step = 16
+
+            def piece(i, inner):
+                at = pl.ds(pl.multiple_of(i * step, step), step)
+                total = None
+                for b in range(DENSITIES):
+                    there = pl.ds(pl.multiple_of(b * own + i * step, step), step)
+                    term = hess[a, b, at, middle_lanes].astype(jnp.float32) * dens[there, middle_lanes]
+                    total = term if total is None else total + term
+                into = pl.ds(pl.multiple_of(a * own + i * step, step), step)
+                lowered[into, middle_lanes] = total.astype(jnp.bfloat16)
+                return inner
+
+            lax.fori_loop(0, own // step, piece, 0)
+            back = lax.dot_general(lowered[part, source], bands[a, target, source],
+                                   (((1,), (1,)), ((), ())), preferred_element_type=jnp.float32)
+            back_high[part, target], back_low[part, target] = split(back)
+            return carry
+
+        lax.fori_loop(0, DENSITIES, body, 0)
 
     def contribute(h, start, count):
         z = pl.ds(h * half, half)
@@ -260,14 +250,6 @@
         for kind, (source, target, device) in enumerate(plan):
             returns[kind, h] = remote(source, target, back_send_sems.at[kind, h], back_recv_sems.at[kind, h], device)
 
-    for h in range(halves):
-        contribute(h, 0, reach)
-        for kind in (0, 1):
-            returns[kind, h].start()
-        contribute(h, reach + span_rows, reach)
-        for kind in (2, 3):
-            returns[kind, h].start()
-
     def strips(h):
         z = pl.ds(h * half, half)
         for kind, rows_at, strip in ((0, first, 6), (2, last, 7)):
@@ -279,13 +261,53 @@
             spread[rows_at, far, z] = spread[rows_at, far, z] + from_right[rows_at, :, z]
             returns[strip, h].start()
 
-    for h in range(halves):
-        strips(h)
-    for h in range(halves):
+    def corners(h):
+        contribute(h, 0, reach)
+        for kind in (0, 1):
+            returns[kind, h].start()
+        contribute(h, reach + span_rows, reach)
+        for kind in (2, 3):
+            returns[kind, h].start()
+
+    def sides(h):
         for start in range(reach, reach + span_rows, reach):
             contribute(h, start, reach)
         for kind in (4, 5):
             returns[kind, h].start()
+
+    relayed = 0
+    ready = 0
+    for h in range(halves):
+        middle(h)
+        if relayed < chunks:
+            relay(relayed)
+            relayed += 1
+    for h in range(halves):
+        need = min(chunks, (h + 1) * per_half + 1)
+        while ready < need:
+            stop = min(need, ready + per_half)
+            while relayed < stop:
+                relay(relayed)
+                relayed += 1
+            edges(ready, stop)
+            ready = stop
+        if relayed < chunks:
+            relay(relayed)
+            relayed += 1
+        begin = h * half
+        source = pl.ds(max(0, begin - LANES), need * LANES - max(0, begin - LANES))
+        fresh = pl.ds(begin, need * LANES - begin)
+        along_depth(source, fresh)
+        if h == 0:
+            fetch.wait()
+        else:
+            strips(h - 1)
+        gradient(fresh, source, pl.ds(begin, half))
+        corners(h)
+        if h > 0:
+            sides(h - 1)
+    strips(halves - 1)
+    sides(halves - 1)
     for h in range(halves):
         z = pl.ds(h * half, half)
         for kind in (4, 5):
@@ -331,7 +353,8 @@
             pltpu.VMEM((wide, DENSITIES * own), bf16),
             pltpu.VMEM((DENSITIES, depth, depth), bf16),
             pltpu.VMEM((DENSITIES, DENSITIES, own, depth), bf16),
-            pltpu.VMEM((own, depth), bf16),
+            pltpu.VMEM((DENSITIES * own, depth), bf16),
+            pltpu.VMEM((DENSITIES * own, depth), f32),
             pltpu.VMEM((DENSITIES * own, depth), f32),
             pltpu.VMEM((DENSITIES * own, depth), bf16),
             pltpu.VMEM((DENSITIES * own, depth), bf16),

time: 53.2 us -> 58.4 us (1.098)
  Pallas kernels: 51.1 us -> 56.3 us
    pallas_call x1, Pallas kernels: 51.1 us -> 56.3 us  [per_device(): pl.pallas_call(lambda *refs: compute(sizes, counts, *refs), out_shape=jax...]
where the time goes in v3:
time: 58.4 us; the launch traced here: 58.2 us
  Pallas kernels  56.3 us (96%)
  local copies, waits for them, and re-layouts  1.88 us (3%)
    pallas_call x1, Pallas kernels, per_device(): pl.pallas_call(lambda *refs: compute(sizes, counts, *refs), out_shape=jax...  56.3 us
    unnamed x1, local copies, waits for them, and re-layouts  1.88 us

profile of v3, /device:TPU:0, one launch (start us, length us, event | category | flops | bytes accessed | tf_op | source)
XLA Modules:
  0.0 58.2 jit_solution(6663145208139429276)
XLA Ops:
  0.0 56.3 %shard_map.55 = f32[16,16,512]{2,1,0:T(8,128)} custom-call(f32[16,16,512]{2,1,0:T(8,128)} %refs_0_.1, bf16[5,5,256,512]{3,2,1,0:T(8,128)(2,1)} %bitcast.1, f32[5,17]{1,0:T(8,128)} %refs_2_.1, f32[5,17]{1,0:T(8,128)} %refs_3_.1, bf16[5,17]{1,0:T(8,128)(2,1)} %refs_4_.1), custom_call_target="tpu_custom_call" | custom-call | tf_op jit(solution)/shard_map/pallas_call | solution.py:337
  56.3 1.9 %copy.7 = f32[16,16,512]{2,1,0:T(8,128)} copy(f32[16,16,512]{2,1,0:T(8,128)} %shard_map.55) | data formatting | bytes 1048576

commit v4 on v3

--- a/solution.py
+++ b/solution.py
@@ -29,7 +29,7 @@
     return total
 
 
-def build_forward(sizes, rows, cols, by_row, by_col, high_ref, low_ref):
+def build_forward(sizes, pieces, rows, cols, by_row, by_col, packed_ref):
     span_rows, span_cols, ext_rows, ext_cols = sizes
     wide = ext_rows * ext_cols
     lane = lax.broadcasted_iota(jnp.int32, (span_rows, wide), 1)
@@ -42,9 +42,11 @@
 
         def body(r, carry):
             high, low = split(by_row[pl.ds(r, 1), :] * by_col[...])
-            start = pl.multiple_of((a * span_rows + r) * span_cols, span_cols)
-            high_ref[pl.ds(start, span_cols), :] = high
-            low_ref[pl.ds(start, span_cols), :] = low
+            at = pl.ds(pl.multiple_of((a * span_rows + r) * span_cols, span_cols), span_cols)
+            for offset, length, begin in pieces:
+                for copy, value in enumerate((high, high, low)):
+                    start = 3 * offset[0] + copy * offset[1] + offset[2]
+                    packed_ref[at, start : start + length] = value[:, begin : begin + length]
             return carry
 
         lax.fori_loop(0, span_rows, body, 0)
@@ -88,13 +90,16 @@
 
 
 def compute(sizes, counts, tangent_ref, hess_ref, rows_ref, cols_ref, depth_ref, out_ref,
-            ext, high, low, by_row, by_col, by_row_t, by_col_t, fwd_high, fwd_low, bwd_high, bwd_low,
+            ext, parts, by_row, by_col, by_row_t, by_col_t, fwd, bwd_high, bwd_low,
             bands, hess, lowered, acc, dens, back_high, back_low, spread, from_left, from_right,
             from_up, from_down, local_sems, send_sems, recv_sems, back_send_sems, back_recv_sems):
     span_rows, span_cols, ext_rows, ext_cols = sizes
     depth = acc.shape[1]
     reach = RADIUS
     own, wide = span_rows * span_cols, ext_rows * ext_cols
+    edge, inner = reach * ext_cols, span_rows * ext_cols
+    pieces = (((0, inner, 0), inner, edge), ((inner, 2 * edge, 0), edge, 0),
+              ((inner, 2 * edge, edge), edge, edge + inner))
     gx, gy = lax.axis_index("gx"), lax.axis_index("gy")
     up = {"gx": lax.rem(gx + counts[0] - 1, counts[0])}
     down = {"gx": lax.rem(gx + 1, counts[0])}
@@ -111,10 +116,6 @@
     barrier = pltpu.get_barrier_semaphore()
     for neighbour in (up, down, left, right):
         pl.semaphore_signal(barrier, inc=1, device_id=neighbour, device_id_type=mesh_ids)
-    rows, cols = rows_ref[...], cols_ref[...]
-    build_forward(sizes, rows, cols, by_row, by_col, fwd_high, fwd_low)
-    build_bands(depth_ref[...].astype(jnp.float32), bands)
-    build_backward(sizes, rows, cols, by_row_t, by_col_t, bwd_high, bwd_low)
     pl.semaphore_wait(barrier, 4)
 
     first, last = pl.ds(0, reach), pl.ds(reach + span_rows, reach)
@@ -155,29 +156,28 @@
         for kind in (4, 5, 6, 7):
             copies[kind, c].start()
 
+    rows, cols = rows_ref[...], cols_ref[...]
+    build_forward(sizes, pieces, rows, cols, by_row, by_col, fwd)
+    build_bands(depth_ref[...].astype(jnp.float32), bands)
+    build_backward(sizes, rows, cols, by_row_t, by_col_t, bwd_high, bwd_low)
     home.wait()
 
     halves = max(1, depth // 256)
     half = depth // halves
     per_half = chunks // halves
-    edge = reach * ext_cols
-
-    def prepare(z, start, count):
-        block = ext[pl.ds(start, count), :, z].reshape(count * ext_cols, z.size)
-        at = pl.ds(start * ext_cols, count * ext_cols)
-        high[at, z], low[at, z] = split(block)
-
-    def lateral(z, ranges, fresh):
+
+    def prepare(z, piece):
+        offset, length, begin = piece
+        block = ext[pl.ds(begin // ext_cols, length // ext_cols), :, z].reshape(length, z.size)
+        high, low = split(block)
+        for copy, value in enumerate((high, low, high)):
+            parts[pl.ds(3 * offset[0] + copy * offset[1] + offset[2], length), z] = value
+
+    def lateral(z, start, length, fresh):
         def body(a, carry):
             part = pl.ds(pl.multiple_of(a * own, own), own)
-            total = None if fresh else acc[part, z]
-            for start, count in ranges:
-                at = pl.ds(start, count)
-                lead = fwd_high[part, at]
-                piece = (dot(lead, high[at, z]) + dot(lead, low[at, z])
-                         + dot(fwd_low[part, at], high[at, z]))
-                total = piece if total is None else total + piece
-            acc[part, z] = total
+            total = dot(fwd[part, pl.ds(start, length)], parts[pl.ds(start, length), z])
+            acc[part, z] = total if fresh else acc[part, z] + total
             return carry
 
         lax.fori_loop(0, DENSITIES, body, 0)
@@ -187,17 +187,17 @@
             copies[2, c].wait_recv()
             copies[3, c].wait_recv()
         z = pl.ds(h * half, half)
-        prepare(z, reach, span_rows)
-        lateral(z, [(edge, span_rows * ext_cols)], True)
+        prepare(z, pieces[0])
+        lateral(z, 0, 3 * inner, True)
 
     def edges(begin, end):
         for c in range(begin, end):
             for kind in (4, 5, 6, 7):
                 copies[kind, c].wait_recv()
         z = pl.ds(begin * LANES, (end - begin) * LANES)
-        prepare(z, 0, reach)
-        prepare(z, reach + span_rows, reach)
-        lateral(z, [(0, edge), (edge + span_rows * ext_cols, edge)], False)
+        prepare(z, pieces[1])
+        prepare(z, pieces[2])
+        lateral(z, 3 * inner, 6 * edge, False)
 
     def along_depth(source, target):
         def body(a, carry):
@@ -208,22 +208,27 @@
         lax.fori_loop(0, DENSITIES, body, 0)
 
     def gradient(middle_lanes, source, target):
+        step = 16
+
+        def piece(i, carry):
+            at = pl.ds(pl.multiple_of(i * step, step), step)
+            for lane in range(middle_lanes.start, middle_lanes.start + middle_lanes.size, LANES):
+                z = pl.ds(lane, LANES)
+                values = [dens[pl.ds(pl.multiple_of(b * own + i * step, step), step), z]
+                          for b in range(DENSITIES)]
+                for a in range(DENSITIES):
+                    total = None
+                    for b in range(DENSITIES):
+                        term = hess[a, b, at, z].astype(jnp.float32) * values[b]
+                        total = term if total is None else total + term
+                    into = pl.ds(pl.multiple_of(a * own + i * step, step), step)
+                    lowered[into, z] = total.astype(jnp.bfloat16)
+            return carry
+
+        lax.fori_loop(0, own // step, piece, 0)
+
         def body(a, carry):
             part = pl.ds(pl.multiple_of(a * own, own), own)
-            step = 16
-
-            def piece(i, inner):
-                at = pl.ds(pl.multiple_of(i * step, step), step)
-                total = None
-                for b in range(DENSITIES):
-                    there = pl.ds(pl.multiple_of(b * own + i * step, step), step)
-                    term = hess[a, b, at, middle_lanes].astype(jnp.float32) * dens[there, middle_lanes]
-                    total = term if total is None else total + term
-                into = pl.ds(pl.multiple_of(a * own + i * step, step), step)
-                lowered[into, middle_lanes] = total.astype(jnp.bfloat16)
-                return inner
-
-            lax.fori_loop(0, own // step, piece, 0)
             back = lax.dot_general(lowered[part, source], bands[a, target, source],
                                    (((1,), (1,)), ((), ())), preferred_element_type=jnp.float32)
             back_high[part, target], back_low[part, target] = split(back)
@@ -276,38 +281,26 @@
             returns[kind, h].start()
 
     relayed = 0
-    ready = 0
     for h in range(halves):
         middle(h)
         if relayed < chunks:
             relay(relayed)
             relayed += 1
-    for h in range(halves):
-        need = min(chunks, (h + 1) * per_half + 1)
-        while ready < need:
-            stop = min(need, ready + per_half)
-            while relayed < stop:
-                relay(relayed)
-                relayed += 1
-            edges(ready, stop)
-            ready = stop
-        if relayed < chunks:
-            relay(relayed)
-            relayed += 1
-        begin = h * half
-        source = pl.ds(max(0, begin - LANES), need * LANES - max(0, begin - LANES))
-        fresh = pl.ds(begin, need * LANES - begin)
-        along_depth(source, fresh)
-        if h == 0:
-            fetch.wait()
-        else:
-            strips(h - 1)
-        gradient(fresh, source, pl.ds(begin, half))
+    while relayed < chunks:
+        relay(relayed)
+        relayed += 1
+    for h in range(halves):
+        edges(h * per_half, (h + 1) * per_half)
+    every = pl.ds(0, depth)
+    along_depth(every, every)
+    fetch.wait()
+    gradient(every, every, every)
+    for h in range(halves):
         corners(h)
-        if h > 0:
-            sides(h - 1)
-    strips(halves - 1)
-    sides(halves - 1)
+    for h in range(halves):
+        strips(h)
+    for h in range(halves):
+        sides(h)
     for h in range(halves):
         z = pl.ds(h * half, half)
         for kind in (4, 5):
@@ -341,14 +334,12 @@
         out_specs=full,
         scratch_shapes=[
             pltpu.VMEM((ext_rows, ext_cols, depth), f32),
-            pltpu.VMEM((wide, depth), bf16),
-            pltpu.VMEM((wide, depth), bf16),
+            pltpu.VMEM((3 * wide, depth), bf16),
             pltpu.VMEM((span_rows, wide), f32),
             pltpu.VMEM((span_cols, wide), f32),
             pltpu.VMEM((ext_rows, DENSITIES * own), f32),
             pltpu.VMEM((ext_cols, DENSITIES * own), f32),
-            pltpu.VMEM((DENSITIES * own, wide), bf16),
-            pltpu.VMEM((DENSITIES * own, wide), bf16),
+            pltpu.VMEM((DENSITIES * own, 3 * wide), bf16),
             pltpu.VMEM((wide, DENSITIES * own), bf16),
             pltpu.VMEM((wide, DENSITIES * own), bf16),
             pltpu.VMEM((DENSITIES, depth, depth), bf16),

time: 58.4 us -> 50.3 us (0.86)
  Pallas kernels: 56.3 us -> 48.3 us
    pallas_call x1, Pallas kernels: 56.3 us -> 48.3 us  [per_device(): pl.pallas_call(lambda *refs: compute(sizes, counts, *refs), out_shape=jax...]
where the time goes in v4:
time: 50.3 us; the launch traced here: 50.2 us
  Pallas kernels  48.3 us (96%)
  local copies, waits for them, and re-layouts  1.88 us (4%)
    pallas_call x1, Pallas kernels, per_device(): pl.pallas_call(lambda *refs: compute(sizes, counts, *refs), out_shape=jax...  48.3 us
    unnamed x1, local copies, waits for them, and re-layouts  1.88 us

profile of v4, /device:TPU:0, one launch (start us, length us, event | category | flops | bytes accessed | tf_op | source)
XLA Modules:
  0.0 50.2 jit_solution(13401645869290446771)
XLA Ops:
  0.0 48.3 %shard_map.55 = f32[16,16,512]{2,1,0:T(8,128)} custom-call(f32[16,16,512]{2,1,0:T(8,128)} %refs_0_.1, bf16[5,5,256,512]{3,2,1,0:T(8,128)(2,1)} %bitcast.1, f32[5,17]{1,0:T(8,128)} %refs_2_.1, f32[5,17]{1,0:T(8,128)} %refs_3_.1, bf16[5,17]{1,0:T(8,128)(2,1)} %refs_4_.1), custom_call_target="tpu_custom_call" | custom-call | tf_op jit(solution)/shard_map/pallas_call | solution.py:330
  48.3 1.9 %copy.7 = f32[16,16,512]{2,1,0:T(8,128)} copy(f32[16,16,512]{2,1,0:T(8,128)} %shard_map.55) | data formatting | bytes 1048576
